TPU v7x, 256 devices: a whole 4x4x8 slice. The times are simulated.
256 devices in a mesh: grp: 2 (over y_hi), dp: 16 (over y_lo, z), tp: 8 (over x, core).
Axes of the slice: x: 4, y: 4 (y_hi: 2, y_lo: 2; y = y_hi * 2 + y_lo), z: 8, core: 2. Of those that a mesh axis runs over, the one named last changes fastest.
Arguments:
- tiers: bfloat16 [2048, 24576], P('dp', ('grp', 'tp')), may hold values from -6 to 6
- w_merge: bfloat16 [24576, 8192], P(('grp', 'tp'), 'dp'), may hold values from -0.0390625 to 0.0390625
- norm_gain: float32 [8192], P('dp'), may hold values from 0.4 to 1.6
- w_head: bfloat16 [8192, 32000], P('dp', ('grp', 'tp')), may hold values from -0.1875 to 0.1875
- token_ids: int32 [2048], P('dp'), may hold values from 0 to 31999
- labels: int32 [2048], P('dp'), may hold values from 0 to 7
- quotas: int32 [8], replicated, may hold values from 64 to 191
Outputs:
- normed: bfloat16 [2048, 8192], P(('grp', 'tp'), 'dp')
- row_loss: float32 [2048], P('dp')
All inputs are finite; a program needn't handle non-finite values.
Results may differ from a plain program's by a relative error of at most 0.008.
Values may be sent and summed in bfloat16 or wider, within the bound.
A program may use at most 64 MiB of HBM per device.

v0:
```python
import jax
import jax.numpy as jnp
from jax import lax
from jax.sharding import PartitionSpec as P

D = 8192
DOMAINS = 8


def sent_to_all(x, axis):
    copies = jnp.broadcast_to(x, (lax.axis_size(axis), *x.shape))
    return lax.all_to_all(copies, axis, split_axis=0, concat_axis=0, tiled=True)


def taken_together(x, axis):
    everything = sent_to_all(x, axis)
    return jnp.sum(everything, axis=0)


def laid_out(pieces, dim):
    lengths = list(pieces.shape[1:])
    lengths[dim] *= pieces.shape[0]
    return jnp.moveaxis(pieces, 0, dim).reshape(lengths)


def gather_directly(x, axis, dim):
    pieces = sent_to_all(x, axis)
    return laid_out(pieces, dim)


def packed_total(arrays, axis):
    flat, at, finished = (jnp.concatenate([a.reshape(-1) for a in arrays]), 0, [])
    total = taken_together(flat, axis)
    for a in arrays:
        finished.append(total[at : at + a.size].reshape(a.shape))
        at += a.size
    return tuple(finished)


def joined_by_halves(pieces, combine):
    while len(jax.tree.leaves(pieces)[0]) > 1:
        pieces = jax.vmap(combine)(*(pieces[side::2] for side in (0, 1)))
    return pieces[0]


def prefix(x, axis, combine, identity):
    length, place = (lax.axis_size(axis), lax.axis_index(axis))
    passed = jnp.arange(length) < place

    def kept(part, zero, own):
        part = jnp.where(
            passed.reshape(-1, *(1 for _ in own.shape)), part, jnp.asarray(zero, own.dtype)
        )
        return part

    pieces = sent_to_all(x, axis)
    return joined_by_halves(kept(pieces, identity, x), combine)


def on_device(tiers, w_merge, norm_gain, w_head, token_ids, labels, quotas):
    partial_value = jnp.dot(
        lax.all_gather(tiers, "dp", axis=0, tiled=True), w_merge, preferred_element_type=jnp.float32
    )
    merged = lax.psum_scatter(partial_value, ("grp", "tp"), scatter_dimension=0, tiled=True)
    squares = taken_together(jnp.sum(merged * merged, axis=1), "dp")
    normed = (merged * lax.rsqrt(squares / D + 1e-05)[:, None] * norm_gain[None, :]).astype(
        jnp.bfloat16
    )
    partial_logits = jnp.dot(
        gather_directly(normed, ("grp", "tp"), 0), w_head, preferred_element_type=jnp.float32
    )
    logits = lax.psum_scatter(
        partial_logits.astype(jnp.bfloat16), "dp", scatter_dimension=0, tiled=True
    ).astype(jnp.float32)
    vocab_local = w_head.shape[1]
    offset = lax.axis_index(("grp", "tp")) * vocab_local
    columns = offset + jnp.arange(vocab_local, dtype=jnp.int32)
    hit = token_ids[:, None] == columns[None, :]
    sumexp_local = jnp.sum(jnp.exp(logits), axis=1)
    target_local = jnp.sum(jnp.where(hit, logits, jnp.float32(0.0)), axis=1)
    sumexp, target = packed_total((sumexp_local, target_local), ("grp", "tp"))
    loss = jnp.log(sumexp) - target
    onehot = (labels[:, None] == jnp.arange(DOMAINS, dtype=jnp.int32)[None, :]).astype(jnp.int32)
    local_counts = jnp.sum(onehot, axis=0)
    before = prefix(
        local_counts, "dp", lambda first, second: first + second, jnp.zeros((DOMAINS,), jnp.int32)
    )
    earlier = jnp.cumsum(onehot, axis=0) - onehot + before[None, :]
    rank = jnp.sum(earlier * onehot, axis=1)
    allowed = jnp.sum(onehot * quotas[None, :], axis=1)
    row_loss = jnp.where(rank < allowed, loss, jnp.float32(0.0))
    return (normed, row_loss)


def solution(mesh):
    in_specs = (
        P("dp", ("grp", "tp")),
        P(("grp", "tp"), "dp"),
        P("dp"),
        P("dp", ("grp", "tp")),
        P("dp"),
        P("dp"),
        P(),
    )
    out_specs = (P(("grp", "tp"), "dp"), P("dp"))
    return jax.shard_map(
        on_device, mesh=mesh, in_specs=in_specs, out_specs=out_specs, check_vma=False
    )
```

profile of v0, /device:TPU:1, one launch (start us, length us, event | category | flops | bytes accessed | tf_op | source)
XLA Modules:
  0.0 378.2 jit_solution(561111012788503821)
XLA Ops:
  7.2 0.7 all-gather.2.cloned.1.call-update
  8.0 84.2 %all-gather.2.cloned.1.call-done = bf16[2048,1536]{1,0:T(8,128)(2,1)} async-done(((bf16[128,1536]{1,0:T(8,128)(2,1)}), bf16[2048,1536]{1,0:T(8,128)(2,1)}) %all-gather.2.cloned.1.call-update) | async-done | bytes 6291472 | tf_op jit(solution)/shard_map/all_gather | solution.py:62
  92.2 8.7 %fusion.4 = f32[2048,512]{1,0:T(8,128)} fusion(bf16[2048,1536]{1,0:T(8,128)(2,1)} %all-gather.2.cloned.1.call-done, bf16[1536,512]{1,0:T(8,128)(2,1)} %param.8), kind=kOutput, calls=%fused_computation.19 | convolution fusion | flops 3221225472 | bytes 12058624 | tf_op jit(solution)/shard_map/dot_general | solution.py:61
  100.9 87.9 %reduce-scatter.5.cloned.1.call-done = f32[128,512]{1,0:T(8,128)} async-done(((f32[2048,512]{1,0:T(8,128)}), f32[128,512]{1,0:T(8,128)}) %reduce-scatter.5.cloned.1.call-update) | async-done | bytes 262160 | tf_op jit(solution)/shard_map/reduce_scatter | solution.py:64
  188.9 1.1 multiply_reduce_fusion
  190.0 14.0 %all_to_all.26 = f32[16,1,128]{2,1,0:T(1,128)S(1)} all-to-all(f32[16,1,128]{2,1,0:T(1,128)S(1)} %broadcast_in_dim.39), channel_id=1, replica_groups=mesh['grp'=2,'dp'=16,'tp'=8] {'dp'}, dimensions={0} | all-to-all | bytes 16384 | tf_op jit(solution)/shard_map/all_to_all | solution.py:12
  204.0 1.0 multiply_convert_fusion
  205.0 0.2 broadcast_in_dim.43
  205.2 36.7 %all_to_all.27 = bf16[16,128,512]{2,1,0:T(8,128)(2,1)S(1)} all-to-all(bf16[16,128,512]{2,1,0:T(8,128)(2,1)S(1)} %broadcast_in_dim.43), channel_id=1, replica_groups=mesh['grp'=2,'dp'=16,'tp'=8] {'grp','tp'}, dimensions={0} | all-to-all | bytes 4194304 | tf_op jit(solution)/shard_map/all_to_all | solution.py:12
  242.0 6.6 %convolution_convert_fusion = bf16[2048,2000]{0,1:T(8,128)(2,1)} fusion(bf16[2048,512]{1,0:T(8,128)(2,1)S(1)} %bitcast.9, bf16[512,2000]{0,1:T(8,128)(2,1)S(1)} %copy-done), kind=kOutput, calls=%fused_computation | convolution fusion | flops 4198400000 | bytes 12337152 | tf_op jit(solution)/shard_map/dot_general | solution.py:69
  248.5 12.3 %copy.14 = bf16[2048,2000]{1,0:T(8,128)(2,1)} copy(bf16[2048,2000]{0,1:T(8,128)(2,1)} %convolution_convert_fusion) | data formatting | bytes 16384000
  260.9 0.6 copy-done.3
  261.6 0.6 broadcast_in_dim.41
  262.2 3.4 all-to-all-start.1
  265.9 6.8 %all-to-all-done.1 = s32[16,1,8]{2,1,0:T(1,128)S(1)} async-done(((s32[16,1,8]{2,1,0:T(1,128)}), s32[16,1,8]{2,1,0:T(1,128)S(1)}, u32[]{:S(2)}, u32[]{:S(2)}) %all-to-all-start.1) | async-done | bytes 544 | tf_op jit(solution)/shard_map/all_to_all | solution.py:12
  273.3 0.2 add_reduce_fusion
  273.5 81.0 %reduce-scatter.7.cloned.1.call-done = bf16[128,2000]{1,0:T(8,128)(2,1)} async-done(((bf16[2048,2000]{1,0:T(8,128)(2,1)}), bf16[128,2000]{1,0:T(8,128)(2,1)}) %reduce-scatter.7.cloned.1.call-update) | async-done | bytes 512016
  354.6 1.3 copy.15
  355.9 0.4 fusion
  356.3 0.6 broadcast_in_dim.45
  356.9 6.9 %all-to-all-start.3 = ((f32[16,1,256]{2,1,0:T(1,128)}), f32[16,1,256]{2,1,0:T(1,128)S(1)}, u32[]{:S(2)}, u32[]{:S(2)}) async-start(f32[16,1,256]{2,1,0:T(1,128)} %broadcast_in_dim.45), calls=%async_computation.4 | async-start | bytes 32768 | tf_op jit(solution)/shard_map/all_to_all | solution.py:12
  363.8 0.2 select_reduce_fusion
  364.0 7.1 %all-to-all-done.3 = f32[16,1,256]{2,1,0:T(1,128)S(1)} async-done(((f32[16,1,256]{2,1,0:T(1,128)}), f32[16,1,256]{2,1,0:T(1,128)S(1)}, u32[]{:S(2)}, u32[]{:S(2)}) %all-to-all-start.3) | async-done | bytes 16416 | tf_op jit(solution)/shard_map/all_to_all | solution.py:12
  371.1 0.5 compare_select_fusion
  (37 shorter events, 1.2 us)
Async XLA Ops:
  7.2 234.8 %copy-start = (bf16[512,2000]{0,1:T(8,128)(2,1)S(1)}, bf16[512,2000]{0,1:T(8,128)(2,1)}, u32[]{:S(2)}) copy-start(bf16[512,2000]{0,1:T(8,128)(2,1)} %param.10) | copy-start | bytes 6144004
  7.2 85.0 %all-gather.2.cloned.1.call-start = ((), (), s32[]{:S(2)}) async-start(), calls=%async_computation.6 | async-start | bytes 6684672 | tf_op jit(solution)/shard_map/all_gather | solution.py:62
  7.9 181.0 %reduce-scatter.5.cloned.1.call-start = ((), (), s32[]{:S(2)}) async-start(), calls=%async_computation.7 | async-start | bytes 4456448 | tf_op jit(solution)/shard_map/reduce_scatter | solution.py:64
  100.9 103.1 %copy-start.2 = (f32[512]{0:T(512)S(1)}, f32[512]{0:T(512)}, u32[]{:S(2)}) copy-start(f32[512]{0:T(512)} %param.9) | copy-start | bytes 6148
  100.9 253.7 %reduce-scatter.7.cloned.1.call-start = ((), (), s32[]{:S(2)}) async-start(), calls=%async_computation.8 | async-start | bytes 8912896
  205.0 36.9 %copy-start.1 = (bf16[128,512]{1,0:T(8,128)(2,1)}, bf16[128,512]{1,0:T(8,128)(2,1)S(1)}, u32[]{:S(2)}) copy-start(bf16[128,512]{1,0:T(8,128)(2,1)S(1)} %multiply_convert_fusion) | copy-start | bytes 393220
  260.8 0.7 copy-start.3
  260.8 95.1 %copy-start.4 = (s32[128]{0:T(128)S(1)}, s32[128]{0:T(128)}, u32[]{:S(2)}) copy-start(s32[128]{0:T(128)} %param.11) | copy-start | bytes 1540
  260.8 103.0 %copy-start.5 = (s32[8]{0:T(128)S(1)}, s32[8]{0:T(128)}, u32[]{:S(2)}) copy-start(s32[8]{0:T(128)} %param.13) | copy-start | bytes 100
  262.2 10.6 %all-to-all-start.1 = ((s32[16,1,8]{2,1,0:T(1,128)}), s32[16,1,8]{2,1,0:T(1,128)S(1)}, u32[]{:S(2)}, u32[]{:S(2)}) async-start(s32[16,1,8]{2,1,0:T(1,128)} %broadcast_in_dim.41), calls=%async_computation.2 | async-start | bytes 16384 | tf_op jit(solution)/shard_map/all_to_all | solution.py:12
  356.9 14.2 %all-to-all-start.3 = ((f32[16,1,256]{2,1,0:T(1,128)}), f32[16,1,256]{2,1,0:T(1,128)S(1)}, u32[]{:S(2)}, u32[]{:S(2)}) async-start(f32[16,1,256]{2,1,0:T(1,128)} %broadcast_in_dim.45), calls=%async_computation.4 | async-start | bytes 32768 | tf_op jit(solution)/shard_map/all_to_all | solution.py:12
Sparse Core Ops, SparseCore 0:
  9.8 82.3 all-gather.1
  101.0 87.8 reduce-scatter.4
  261.0 93.5 reduce-scatter.6
where the time goes:
time: 379 us; the launch traced here: 378 us
  waiting for transfers between devices  268 us (71%)
  blocking collectives  50.7 us (13%)
  local copies, waits for them, and re-layouts  16.2 us (4%)
  matrix products  15.2 us (4%)
  between operations  13.9 us (4%)
  starting transfers between devices  10.5 us (3%)
  other arithmetic  3.81 us (1%)
    reduce_scatter x1, waiting for transfers between devices, on_device(): lax.psum_scatter(partial_value, ('grp', 'tp'), scatter_dimension=0, tiled...  87.9 us
    all_gather x1, waiting for transfers between devices, on_device(): lax.all_gather(tiers, 'dp', axis=0, tiled=True)  84.2 us
    unnamed x4, waiting for transfers between devices  81.7 us
    all_to_all x2, blocking collectives, sent_to_all(): return lax.all_to_all(copies, axis, split_axis=0, concat_axis=0, tiled=True)  50.7 us
    unnamed x14, local copies, waits for them, and re-layouts  14.3 us
    all_to_all x2, waiting for transfers between devices, sent_to_all(): return lax.all_to_all(copies, axis, split_axis=0, concat_axis=0, tiled=True)  13.9 us
    all_to_all x2, starting transfers between devices, sent_to_all(): return lax.all_to_all(copies, axis, split_axis=0, concat_axis=0, tiled=True)  10.4 us
    dot_general x1, matrix products, on_device(): jnp.dot(lax.all_gather(tiers, 'dp', axis=0, tiled=True), w_merge, preferr...  8.68 us
  transfers between devices with their start and end apart: 5, of which 5 were waited for; matrix products, arithmetic and copies ran while one was open for 1% of the time, Pallas kernels for 0%

commit v1 on v0

v1 whole, which is shorter than its diff:
```python
import jax
import jax.numpy as jnp
from jax import lax
from jax.experimental import pallas as pl
from jax.experimental.pallas import tpu as pltpu
from jax.sharding import PartitionSpec as P

D = 8192
Z = 8
ROWS = 128
FEAT = 1536
COLS = 512
VOC = 2000
Q = 256
SPLIT = (0, 1008, VOC)
STEP = (336, 496)
N_SEMS = 140


class Net:
    def __init__(self, send, recv):
        self.send, self.recv, self.n, self.started = send, recv, 0, {}

    def make(self, src, dst, device, i):
        return pltpu.make_async_remote_copy(
            src_ref=src,
            dst_ref=dst,
            send_sem=self.send.at[i],
            recv_sem=self.recv.at[i],
            device_id=device,
            device_id_type=pl.DeviceIdType.MESH,
        )

    def put(self, src, dst, device):
        i = self.n
        self.n += 1
        copy = self.make(src, dst, device, i)
        copy.start()
        self.started[i] = copy
        return i, device

    def got(self, handle, dst):
        i, device = handle
        self.make(dst, dst, device, i).wait_recv()

    def sent(self, handles):
        for i, _ in handles:
            self.started.pop(i).wait_send()

    def drain(self):
        for copy in self.started.values():
            copy.wait_send()


def kernel(
    tiers, w_merge, gain, w_head, token_ids, labels, quotas,
    normed_out, loss_out,
    T, W, G, WH, LA, S1, R1, K, S2, R2, S3, R3, MG, SQ, N, OR, ES, ER, PB, FB, FR,
    send, recv, local, cross,
):
    g, d, t = (lax.axis_index(a) for a in ("grp", "dp", "tp"))
    yl, z = lax.div(d, Z), lax.rem(d, Z)
    x, c = lax.div(t, 2), lax.rem(t, 2)
    net = Net(send, recv)

    def at_z(step):
        return lax.rem(z + step + 2 * Z, Z)

    def slot(b):
        return lax.rem(b, 2), lax.div(b, 2)

    ring = [{"dp": yl * Z + at_z(1)}, {"dp": yl * Z + at_z(-1)}]
    y_peer = {"dp": (1 - yl) * Z + z}
    core_peer = {"tp": 2 * x + 1 - c}
    grp_peer = {"grp": 1 - g}

    def x_to(o):
        return lax.rem(x + o + 4, 4)

    def x_peer(o):
        return {"tp": 2 * x_to(o) + c}

    keep_local = [
        pltpu.make_async_copy(tiers, T.at[slot(z)], local.at[0]),
        pltpu.make_async_copy(w_merge, W.at[yl], local.at[1]),
        pltpu.make_async_copy(w_head, WH.at[yl], local.at[2]),
    ]
    tier_in = {}

    def half(h):
        return pl.ds(64 * h, 64)

    for h in (0, 1):
        for way in (0, 1):
            tier_in[way, 1, h] = net.put(
                tiers.at[half(h)], T.at[(*slot(z), half(h))], ring[way]
            )
    keep_local[0].start()
    keep_local[1].start()
    w_in = []
    for q in (0, 1):
        cols = pl.ds(Q * q, Q)
        w_in.append(net.put(w_merge.at[:, cols], W.at[yl, :, cols], y_peer))
    G[yl] = jnp.broadcast_to(gain[...], (8, COLS))
    gain_in = net.put(G.at[yl], G.at[yl], y_peer)
    LA[d] = jnp.broadcast_to(labels[...], (8, ROWS))
    label_in = []
    for o in range(1, 16):
        label_in.append(net.put(LA.at[d], LA.at[d], {"dp": lax.rem(d + o, 16)}))
    keep_local[2].start()

    for s in (1, 2, 3, 4):
        for h in (0, 1):
            for way in (0, 1):
                if (way, s, h) not in tier_in:
                    continue
                origin = at_z(-s if way == 0 else s)
                piece = T.at[(*slot(origin), half(h))]
                net.got(tier_in[way, s, h], piece)
                if s < 3 or (s == 3 and h == way):
                    tier_in[way, s + 1, h] = net.put(piece, piece, ring[way])
    keep_local[0].wait()
    keep_local[1].wait()

    def w_of(q):
        j = yl if q < 2 else 1 - yl
        return W[j, :, pl.ds(Q * (q % 2), Q)]

    def product(p, q):
        a = T[p].reshape(4 * ROWS, FEAT)
        return jnp.dot(a, w_of(q), preferred_element_type=jnp.float32)

    in1, in2, in3 = {}, {}, {}

    def stage1(q):
        S1[q] = product(1 - c, q).astype(jnp.bfloat16)
        in1[q] = net.put(S1.at[q], R1.at[q], core_peer)
        K[q] = product(c, q)

    def stage2(q):
        net.got(in1[q], R1.at[q])
        total = K[q] + R1[q].astype(jnp.float32)
        K[q] = total
        S2[q] = total.astype(jnp.bfloat16)
        for o in (1, 2, 3):
            rows = pl.ds(pl.multiple_of(x_to(o) * ROWS, ROWS), ROWS)
            in2[q, o] = net.put(S2.at[q, rows], R2.at[q, o - 1], x_peer(o))

    def stage3(q):
        total = K[q, pl.ds(pl.multiple_of(x * ROWS, ROWS), ROWS)]
        for o in (1, 2, 3):
            net.got(in2[q, o], R2.at[q, o - 1])
            total += R2[q, o - 1].astype(jnp.float32)
        K[q, 0:ROWS] = total
        S3[q] = total.astype(jnp.bfloat16)
        other = pl.ds(pl.multiple_of((1 - g) * 64, 64), 64)
        in3[q] = net.put(S3.at[q, other], R3.at[q], grp_peer)

    squares = []

    def stage4(q):
        net.got(in3[q], R3.at[q])
        mine = pl.ds(pl.multiple_of(g * 64, 64), 64)
        m = K[q, mine] + R3[q].astype(jnp.float32)
        MG[yl if q < 2 else 1 - yl, :, pl.ds(Q * (q % 2), Q)] = m
        m = m * m
        squares.append(m[:, :128] + m[:, 128:])

    def other_columns():
        for q in (0, 1):
            net.got(w_in[q], W.at[1 - yl, :, pl.ds(Q * q, Q)])

    stage1(0)
    stage1(1)
    stage2(0)
    other_columns()
    stage1(2)
    stage2(1)
    stage3(0)
    stage1(3)
    net.sent(w_in)
    wh_in = []
    for h in (0, 1):
        rows = pl.ds(SPLIT[h], SPLIT[h + 1] - SPLIT[h])
        wh_in.append(net.put(w_head.at[rows], WH.at[yl, rows], y_peer))
    stage2(2)
    stage3(1)
    stage4(0)
    stage2(3)
    stage3(2)
    stage4(1)
    stage3(3)
    stage4(2)
    stage4(3)

    SQ[z] = (squares[0] + squares[1]) + (squares[2] + squares[3])
    sq_in = [
        net.put(SQ.at[z], SQ.at[z], {"dp": yl * Z + at_z(o)}) for o in range(1, Z)
    ]
    net.got(gain_in, G.at[1 - yl])
    for o in range(1, Z):
        net.got(sq_in[o - 1], SQ.at[at_z(-o)])
    total = SQ[0]
    for i in range(1, Z):
        total += SQ[i]
    r = lax.rsqrt(jnp.sum(total, axis=1, keepdims=True) / D + 1e-05)

    def part(i, mine, p=c):
        row = g if mine else 1 - g
        return N.at[p, i, pl.ds(pl.multiple_of(row * 64, 64), 64)]

    own = pl.ds(pl.multiple_of(g * 64, 64), 64)
    for j in (0, 1):
        N[c, x, own, pl.ds(COLS * j, COLS)] = (MG[j] * r * G[j, 0:1, :]).astype(
            jnp.bfloat16
        )
    grp_in = net.put(part(x, True), part(x, True), grp_peer)
    x_in, core_in = {}, {}
    for o in (1, 2, 3):
        x_in[o, 0] = net.put(part(x, True), part(x, True), x_peer(o))
    core_in[0, 0] = net.put(part(x, True), part(x, True), core_peer)
    net.got(grp_in, part(x, False))
    for o in (1, 2, 3):
        x_in[o, 1] = net.put(part(x, False), part(x, False), x_peer(o))
    core_in[0, 1] = net.put(part(x, False), part(x, False), core_peer)

    columns = pl.ds(pl.multiple_of(g * COLS, COLS), COLS)
    block = N.at[c, x, :, columns]
    to_block = pltpu.make_async_remote_copy(
        src_ref=block,
        dst_ref=OR,
        send_sem=cross.at[0],
        recv_sem=cross.at[1],
        device_id={"grp": yl, "dp": g * Z + z},
        device_id_type=pl.DeviceIdType.MESH,
    )

    @pl.when(g != yl)
    def _():
        to_block.start()

    for mine in (0, 1):
        for o in (1, 2, 3):
            piece = part(x_to(-o), mine == 0)
            net.got(x_in[o, mine], piece)
            core_in[o, mine] = net.put(piece, piece, core_peer)
    for o in (0, 1, 2, 3):
        for mine in (0, 1):
            net.got(core_in[o, mine], part(x_to(-o), mine == 0, 1 - c))

    keep_local[2].wait()

    def logits_part(b, h, out):
        p, i = slot(b)

        def body(k, _):
            rows = pl.ds(pl.multiple_of(SPLIT[h] + k * STEP[h], 16), STEP[h])
            total = jnp.zeros((STEP[h], ROWS), jnp.float32)
            for j in (0, 1):
                total += lax.dot_general(
                    WH[j, rows, :],
                    N[p, i, :, pl.ds(COLS * j, COLS)],
                    (((1,), (1,)), ((), ())),
                    preferred_element_type=jnp.float32,
                )
            out[rows, :] = total
            return 0

        lax.fori_loop(0, (SPLIT[h + 1] - SPLIT[h]) // STEP[h], body, 0)

    got_wh = [False, False]
    logit_in = {}
    for s in (4, 3, 2, 1):
        for h in (0, 1):
            rows = pl.ds(SPLIT[h], SPLIT[h + 1] - SPLIT[h])
            if not got_wh[h]:
                net.got(wh_in[h], WH.at[1 - yl, rows])
                got_wh[h] = True
            for way in (0, 1):
                if s == 4 and h != way:
                    continue
                logits_part(at_z(s if way == 0 else -s), h, PB.at[way])
                total = PB[way, rows, :]
                if (way, s + 1, h) in logit_in:
                    net.got(logit_in[way, s + 1, h], ER.at[way, s, rows])
                    total += ER[way, s, rows, :].astype(jnp.float32)
                ES[way, s - 1, rows, :] = total.astype(jnp.bfloat16)
                logit_in[way, s, h] = net.put(
                    ES.at[way, s - 1, rows], ER.at[way, s - 1, rows], ring[way]
                )

    for o in range(1, 16):
        net.got(label_in[o - 1], LA.at[lax.rem(d - o + 16, 16)])
    domain = lax.broadcasted_iota(jnp.int32, (8, ROWS), 0)
    counts = jnp.zeros((8, ROWS), jnp.float32)
    for i in range(16):
        counts += jnp.where((LA[i] == domain) & (i < d), 1.0, 0.0)
    onehot = jnp.where(labels[...] == domain, 1.0, 0.0)
    earlier = jnp.where(
        lax.broadcasted_iota(jnp.int32, (ROWS, ROWS), 0)
        < lax.broadcasted_iota(jnp.int32, (ROWS, ROWS), 1),
        1.0,
        0.0,
    )
    before = jnp.dot(
        onehot.astype(jnp.bfloat16),
        earlier.astype(jnp.bfloat16),
        preferred_element_type=jnp.float32,
    ) + jnp.sum(counts, axis=1, keepdims=True)
    rank = jnp.sum(onehot * before, axis=0, keepdims=True)
    allowed = jnp.zeros((1, ROWS), jnp.int32)
    for e in range(8):
        allowed = jnp.where(labels[...] == e, quotas[e], allowed)

    for h in (0, 1):
        logits_part(z, h, PB.at[0])
    offset = (g * 8 + t) * VOC
    for h in (0, 1):
        rows = pl.ds(SPLIT[h], SPLIT[h + 1] - SPLIT[h])
        for way in (0, 1):
            net.got(logit_in[way, 1, h], ER.at[way, 0, rows])

    def summed(k, sums):
        rows = pl.ds(pl.multiple_of(k * 80, 16), 80)
        v = PB[0, rows, :] + ER[0, 0, rows, :].astype(jnp.float32)
        v += ER[1, 0, rows, :].astype(jnp.float32)
        index = offset + k * 80 + lax.broadcasted_iota(jnp.int32, (80, ROWS), 0)
        hit = jnp.where(index == token_ids[...], v, 0.0)
        e = jnp.exp(v)
        return (
            sums[0] + jnp.sum(e.reshape(10, 8, ROWS), axis=0),
            sums[1] + jnp.sum(hit.reshape(10, 8, ROWS), axis=0),
        )

    zero = jnp.zeros((8, ROWS), jnp.float32)
    sums = lax.fori_loop(0, VOC // 80, summed, (zero, zero))
    sumexp, target = (jnp.sum(v, axis=0, keepdims=True) for v in sums)
    pair = jnp.where(domain < 4, sumexp, target)

    FB[0] = pair
    i = net.put(FB.at[0], FR.at[0], core_peer)
    net.got(i, FR.at[0])
    pair = pair + FR[0]
    FR[1 + x] = pair
    FB[1] = pair
    pair_in = [net.put(FB.at[1], FR.at[1 + x], x_peer(o)) for o in (1, 2, 3)]
    for o in (1, 2, 3):
        net.got(pair_in[o - 1], FR.at[1 + x_to(-o)])
    pair = (FR[1] + FR[2]) + (FR[3] + FR[4])
    FB[2] = pair
    i = net.put(FB.at[2], FR.at[5], grp_peer)
    net.got(i, FR.at[5])
    pair = pair + FR[5]
    loss = jnp.log(pair[0:1]) - pair[4:5]
    loss_out[...] = jnp.where(rank < allowed.astype(jnp.float32), loss, 0.0)

    @pl.when(g != yl)
    def _():
        to_block.wait_send()
        to_block.wait_recv()
        normed_out[...] = OR[...]

    @pl.when(g == yl)
    def _():
        normed_out[...] = N[c, x, :, columns]

    net.drain()


def on_device(tiers, w_merge, norm_gain, w_head, token_ids, labels, quotas):
    f32, bf16, i32 = jnp.float32, jnp.bfloat16, jnp.int32
    vmem = pl.BlockSpec(memory_space=pltpu.VMEM)
    hbm = pl.BlockSpec(memory_space=pl.ANY)
    normed, loss = pl.pallas_call(
        kernel,
        out_shape=(
            jax.ShapeDtypeStruct((ROWS, COLS), bf16),
            jax.ShapeDtypeStruct((1, ROWS), f32),
        ),
        in_specs=[
            hbm, hbm, vmem, hbm, vmem, vmem, pl.BlockSpec(memory_space=pltpu.SMEM),
        ],
        out_specs=(vmem, vmem),
        scratch_shapes=[
            pltpu.VMEM((2, 4, ROWS, FEAT), bf16),
            pltpu.VMEM((2, FEAT, COLS), bf16),
            pltpu.VMEM((2, 8, COLS), f32),
            pltpu.VMEM((2, VOC, COLS), bf16),
            pltpu.VMEM((16, 8, ROWS), i32),
            pltpu.VMEM((4, 4 * ROWS, Q), bf16),
            pltpu.VMEM((4, 4 * ROWS, Q), bf16),
            pltpu.VMEM((4, 4 * ROWS, Q), f32),
            pltpu.VMEM((4, 4 * ROWS, Q), bf16),
            pltpu.VMEM((4, 3, ROWS, Q), bf16),
            pltpu.VMEM((4, ROWS, Q), bf16),
            pltpu.VMEM((4, 64, Q), bf16),
            pltpu.VMEM((2, 64, COLS), f32),
            pltpu.VMEM((Z, 64, 128), f32),
            pltpu.VMEM((2, 4, ROWS, 2 * COLS), bf16),
            pltpu.VMEM((ROWS, COLS), bf16),
            pltpu.VMEM((2, 4, VOC, ROWS), bf16),
            pltpu.VMEM((2, 4, VOC, ROWS), bf16),
            pltpu.VMEM((2, VOC, ROWS), f32),
            pltpu.VMEM((3, 8, ROWS), f32),
            pltpu.VMEM((6, 8, ROWS), f32),
            pltpu.SemaphoreType.DMA((N_SEMS,)),
            pltpu.SemaphoreType.DMA((N_SEMS,)),
            pltpu.SemaphoreType.DMA((3,)),
            pltpu.SemaphoreType.DMA((2,)),
        ],
        compiler_params=pltpu.CompilerParams(
            has_side_effects=True, vmem_limit_bytes=56 * 2**20
        ),
    )(
        tiers,
        w_merge,
        norm_gain.reshape(1, COLS),
        w_head.T,
        token_ids.reshape(1, ROWS),
        labels.reshape(1, ROWS),
        quotas,
    )
    return normed, loss.reshape(ROWS)


def solution(mesh):
    both = ("grp", "tp")
    in_specs = (
        P("dp", both),
        P(both, "dp"),
        P("dp"),
        P("dp", both),
        P("dp"),
        P("dp"),
        P(),
    )
    out_specs = (P(both, "dp"), P("dp"))
    return jax.shard_map(
        on_device, mesh=mesh, in_specs=in_specs, out_specs=out_specs, check_vma=False
    )
```

time: 379 us -> 192 us (0.51)
  waiting for transfers between devices: 268 us -> 0 us
  Pallas kernels: 0 us -> 187 us
  blocking collectives: 50.7 us -> 0 us
  matrix products: 15.2 us -> 0 us
  local copies, waits for them, and re-layouts: 16.2 us -> 2.74 us
  between operations: 13.9 us -> 0.64 us
  starting transfers between devices: 10.5 us -> 0 us
  other arithmetic: 3.81 us -> 0 us
    pallas_call x0 -> x1, Pallas kernels: none -> 187 us  [on_device(): pl.pallas_call(kernel, out_shape=(jax.ShapeDtypeStruct((ROWS, COLS), bf16...]
    reduce_scatter x1 -> x0, waiting for transfers between devices: 87.9 us -> none  [on_device(): lax.psum_scatter(partial_value, ('grp', 'tp'), scatter_dimension=0, tiled...]
    all_gather x1 -> x0, waiting for transfers between devices: 84.2 us -> none  [on_device(): lax.all_gather(tiers, 'dp', axis=0, tiled=True)]
    unnamed x4 -> x0, waiting for transfers between devices: 81.7 us -> none
    all_to_all x2 -> x0, blocking collectives: 50.7 us -> none  [sent_to_all(): return lax.all_to_all(copies, axis, split_axis=0, concat_axis=0, tiled=True)]
    dot_general x2 -> x0, matrix products: 15.2 us -> none  [the longest x1 8.68 us: on_device(): jnp.dot(lax.all_gather(tiers, 'dp', axis=0, tiled=True), w_merge, preferr...]
    all_to_all x2 -> x0, waiting for transfers between devices: 13.9 us -> none  [sent_to_all(): return lax.all_to_all(copies, axis, split_axis=0, concat_axis=0, tiled=True)]
    unnamed x14 -> x2, local copies, waits for them, and re-layouts: 14.3 us -> 2.74 us
  transfers between devices with their start and end apart: 5 -> 0, of which waited for: 5 -> 0; matrix products, arithmetic and copies ran while one was open for 1% -> 0% of each run, Pallas kernels for 0% -> 0%
where the time goes in v1:
time: 192 us; the launch traced here: 191 us
  Pallas kernels  187 us (97%)
  local copies, waits for them, and re-layouts  2.74 us (1%)
    pallas_call x1, Pallas kernels, on_device(): pl.pallas_call(kernel, out_shape=(jax.ShapeDtypeStruct((ROWS, COLS), bf16...  187 us

profile of v1, /device:TPU:1, one launch (start us, length us, event | category | flops | bytes accessed | tf_op | source)
XLA Modules:
  0.0 190.8 jit_solution(6655659697973435349)
XLA Ops:
  0.6 187.4 %shard_map.86 = (bf16[128,512]{1,0:T(8,128)(2,1)}, f32[1,128]{1,0:T(1,128)}) custom-call(bf16[128,1536]{1,0:T(8,128)(2,1)} %tiers.1, bf16[1536,512]{1,0:T(8,128)(2,1)} %w_merge.1, f32[1,512]{1,0:T(1,128)} %bitcast.6, bf16[2000,512]{1,0:T(8,128)(2,1)} %bitcast.5, s32[1,128]{1,0:T(1,128)} %bitcast.7, s32[1,128]{1,0:T(1,128)} %bitcast.8, s32[8]{0:T(128)} %quotas.1), custom_call_target="tpu_custom_call" | custom-call | tf_op jit(solution)/shard_map/pallas_call | solution.py:374
  188.1 1.6 copy.11
  189.6 1.2 copy.12

commit v2 on v0

v2 whole, which is shorter than its diff:
```python
import jax
import jax.numpy as jnp
from jax import lax
from jax.experimental import pallas as pl
from jax.experimental.pallas import tpu as pltpu
from jax.sharding import PartitionSpec as P

D = 8192
Z = 8
ROWS = 128
FEAT = 1536
COLS = 512
VOC = 2000
MINE = 1008
SHIFT = VOC - MINE
SPLIT = (0, 528, MINE)
PIECES = (0, 272, 528, 768, MINE)
N_SEMS = 140
DISTANCE = (0, 1, -1, 2, -2, 3, -3, 4)
POS = {s: i for i, s in enumerate(DISTANCE)} | {-4: 7}


class Net:
    def __init__(self, send, recv):
        self.send, self.recv, self.n, self.started = send, recv, 0, {}

    def make(self, src, dst, device, i):
        return pltpu.make_async_remote_copy(
            src_ref=src,
            dst_ref=dst,
            send_sem=self.send.at[i],
            recv_sem=self.recv.at[i],
            device_id=device,
            device_id_type=pl.DeviceIdType.MESH,
        )

    def put(self, src, dst, device):
        i = self.n
        self.n += 1
        copy = self.make(src, dst, device, i)
        copy.start()
        self.started[i] = copy
        return i, device

    def got(self, handle, dst):
        i, device = handle
        self.make(dst, dst, device, i).wait_recv()

    def sent(self, handles):
        for i, _ in handles:
            self.started.pop(i).wait_send()

    def drain(self):
        for copy in self.started.values():
            copy.wait_send()


def kernel(
    tiers, w_merge, gain, w_head, token_ids, labels, quotas,
    normed_out, loss_out,
    T, W, G, TK, WH, LA, S1, R1, PP, S2, R2, S3, R3, SA, SQ, CB, RC, N, ES, ER, PB, FB, FR,
    send, recv, local,
):
    f32, bf16 = jnp.float32, jnp.bfloat16
    g, d, t = (lax.axis_index(a) for a in ("grp", "dp", "tp"))
    yl, z = lax.div(d, Z), lax.rem(d, Z)
    x, c = lax.div(t, 2), lax.rem(t, 2)
    net = Net(send, recv)

    def at_z(step):
        return lax.rem(z + step + 2 * Z, Z)

    ring = [{"dp": yl * Z + at_z(1)}, {"dp": yl * Z + at_z(-1)}]
    y_peer = {"dp": (1 - yl) * Z + z}
    y_other = {"grp": 1 - g, "dp": (1 - yl) * Z + z}
    core_peer = {"tp": 2 * x + 1 - c}
    grp_peer = {"grp": 1 - g}

    def x_to(o):
        return lax.rem(x + o + 4, 4)

    def x_peer(o):
        return {"tp": 2 * x_to(o) + c}

    def dp_peer(o):
        return {"dp": lax.rem(d + o, 16)}

    def lines(start, size):
        return pl.ds(pl.multiple_of(start, 16), size)

    barrier = pltpu.get_barrier_semaphore()
    peers = [core_peer, grp_peer, y_other]
    peers += [x_peer(o) for o in (1, 2, 3)] + [dp_peer(o) for o in range(1, 16)]
    for peer in peers:
        pl.semaphore_signal(
            barrier, inc=1, device_id=peer, device_id_type=pl.DeviceIdType.MESH
        )
    own_head = w_head.at[lines(yl * SHIFT, MINE)]
    keep_local = [
        pltpu.make_async_copy(tiers, T.at[0], local.at[0]),
        pltpu.make_async_copy(w_merge, W.at[0], local.at[1]),
        pltpu.make_async_copy(own_head, WH.at[0], local.at[2]),
    ]
    for copy in keep_local:
        copy.start()
    G[0] = jnp.broadcast_to(gain[...], (8, COLS))
    TK[0] = jnp.broadcast_to(token_ids[...], (8, ROWS))
    LA[d] = jnp.broadcast_to(labels[...], (8, ROWS))
    SA[...] = jnp.zeros_like(SA)
    pl.semaphore_wait(barrier, len(peers))

    def half(h):
        return pl.ds(64 * h, 64)

    def from_way(way, s):
        return POS[-s if way == 0 else s]

    tier_in = {}
    for h in (0, 1):
        for way in (0, 1):
            tier_in[way, 1, h] = net.put(
                tiers.at[half(h)], T.at[from_way(way, 1), half(h)], ring[way]
            )
    w_in = []
    for q in (0, 1):
        cols = pl.ds(256 * q, 256)
        w_in.append(net.put(w_merge.at[:, cols], W.at[1, :, cols], y_peer))
    gain_in = net.put(G.at[0], G.at[1], y_peer)
    token_in = net.put(TK.at[0], TK.at[1], y_peer)
    label_in = [net.put(LA.at[d], LA.at[d], dp_peer(o)) for o in range(1, 16)]

    def ring_step(s, h):
        for way in (0, 1):
            if (way, s, h) in tier_in:
                piece = T.at[from_way(way, s), half(h)]
                net.got(tier_in[way, s, h], piece)
                if s < 3 or (s == 3 and h == way):
                    to = T.at[from_way(way, s + 1), half(h)]
                    tier_in[way, s + 1, h] = net.put(piece, to, ring[way])

    batches = {
        "a": (0, 0, 3, 0, COLS),
        "b": (0, 3, 7, 0, COLS),
        "c": (0, 7, 8, 0, COLS),
        "d": (1, 0, 8, 0, 256),
        "e": (1, 0, 8, 256, COLS),
    }
    in1, in2, in3, inx, inc, iny, inf = {}, {}, {}, {}, {}, {}, {}
    mine, others = lines(c * 64, 64), lines((1 - c) * 64, 64)
    strip = lines(c * 64 + x * 16, 16)

    def stage1(k):
        w, p0, p1, c0, c1 = batches[k]
        n = p1 - p0
        a = T[p0:p1].reshape(n * ROWS, FEAT)
        v = jnp.dot(a, W[w, :, c0:c1], preferred_element_type=f32)
        PP[w, p0:p1, :, c0:c1] = v.reshape(n, ROWS, c1 - c0)
        S1[w, p0:p1, :, c0:c1] = PP[w, p0:p1, others, c0:c1].astype(bf16)
        at = (w, pl.ds(p0, n), slice(None), pl.ds(c0, c1 - c0))
        in1[k] = net.put(S1.at[at], R1.at[at], core_peer)

    def stage2(k):
        w, p0, p1, c0, c1 = batches[k]
        at = (w, pl.ds(p0, p1 - p0), slice(None), pl.ds(c0, c1 - c0))
        net.got(in1[k], R1.at[at])
        PP[w, p0:p1, mine, c0:c1] += R1[w, p0:p1, :, c0:c1].astype(f32)
        for o in (1, 2, 3):
            rows = lines(c * 64 + x_to(o) * 16, 16)
            S2[o - 1, w, p0:p1, :, c0:c1] = PP[w, p0:p1, rows, c0:c1].astype(bf16)
            in2[k, o] = net.put(
                S2.at[(o - 1, *at)], R2.at[(o - 1, *at)], x_peer(o)
            )

    def stage3(k):
        w, p0, p1, c0, c1 = batches[k]
        at = (w, pl.ds(p0, p1 - p0), slice(None), pl.ds(c0, c1 - c0))
        v = PP[w, p0:p1, strip, c0:c1]
        for o in (1, 2, 3):
            net.got(in2[k, o], R2.at[(o - 1, *at)])
            v += R2[o - 1, w, p0:p1, :, c0:c1].astype(f32)
        S3[w, p0:p1, :, c0:c1] = v.astype(bf16)
        in3[k] = net.put(S3.at[at], R3.at[at], grp_peer)

    def stage4(k):
        w, p0, p1, c0, c1 = batches[k]
        at = (w, pl.ds(p0, p1 - p0), slice(None), pl.ds(c0, c1 - c0))
        net.got(in3[k], R3.at[at])
        v = S3[w, p0:p1, :, c0:c1].astype(f32) + R3[w, p0:p1, :, c0:c1].astype(f32)
        N[w, p0:p1, strip, c0:c1] = (v * G[w, 0:1, c0:c1]).astype(bf16)
        v = v * v
        fold = sum(v[:, :, i : i + 128] for i in range(0, c1 - c0, 128))
        for p in range(p0, p1):
            SA[at_z(DISTANCE[p])] += fold[p - p0]
        piece = N.at[w, pl.ds(p0, p1 - p0), strip, pl.ds(c0, c1 - c0)]
        for o in (1, 2, 3):
            inx[k, o] = net.put(piece, piece, x_peer(o))

    def rows_of(k, rows, other_w=False):
        w, p0, p1, c0, c1 = batches[k]
        w = 1 - w if other_w else w
        return N.at[w, pl.ds(p0, p1 - p0), rows, pl.ds(c0, c1 - c0)]

    there, there_others = lines(ROWS + c * 64, 64), lines(ROWS + (1 - c) * 64, 64)

    def spread(k):
        for o in (1, 2, 3):
            net.got(inx[k, o], rows_of(k, lines(c * 64 + x_to(-o) * 16, 16)))
        inc[k] = net.put(rows_of(k, mine), rows_of(k, mine), core_peer)
        iny[k] = net.put(rows_of(k, mine), rows_of(k, there, True), y_other)

    def spread2(k):
        net.got(iny[k], rows_of(k, there, True))
        piece = rows_of(k, there, True)
        inf[k] = net.put(piece, piece, core_peer)

    def spread3(k):
        net.got(inc[k], rows_of(k, others))
        net.got(inf[k], rows_of(k, there_others, True))

    wh_in = []

    def head_piece(i):
        rows = lines((1 - yl) * SHIFT + PIECES[i], PIECES[i + 1] - PIECES[i])
        to = WH.at[1, pl.ds(PIECES[i], PIECES[i + 1] - PIECES[i])]
        wh_in.append(net.put(w_head.at[rows], to, y_peer))

    ring_step(1, 0)
    ring_step(1, 1)
    keep_local[0].wait()
    keep_local[1].wait()
    stage1("a")
    ring_step(2, 0)
    stage2("a")
    ring_step(2, 1)
    stage3("a")
    ring_step(3, 0)
    stage4("a")
    ring_step(3, 1)
    stage1("b")
    spread("a")
    ring_step(4, 0)
    ring_step(4, 1)
    stage1("c")
    stage2("b")
    net.got(w_in[0], W.at[1, :, pl.ds(0, 256)])
    stage1("d")
    stage2("c")
    stage3("b")
    net.got(w_in[1], W.at[1, :, pl.ds(256, 256)])
    stage1("e")
    net.sent(w_in)
    head_piece(0)
    stage2("d")
    stage3("c")
    net.got(gain_in, G.at[1])
    stage4("b")
    stage2("e")
    stage3("d")
    stage4("c")
    head_piece(1)
    spread2("a")
    spread("b")
    stage3("e")
    stage4("d")
    spread("c")
    stage4("e")
    head_piece(2)
    spread2("b")
    spread("d")
    spread2("c")

    by_row = SA[...].reshape(ROWS, 128).T
    SQ[z] = jnp.broadcast_to(jnp.sum(by_row, axis=0, keepdims=True), (8, ROWS))
    sq_in = [
        net.put(SQ.at[z], SQ.at[z], {"dp": yl * Z + at_z(o)}) for o in range(1, Z)
    ]
    spread("e")
    head_piece(3)
    spread2("d")
    spread2("e")
    keep_local[2].wait()
    for k in batches:
        spread3(k)

    def logits_part(p, v, out):
        rows = pl.ds(SPLIT[v], SPLIT[v + 1] - SPLIT[v])
        total = None
        for w in (0, 1):
            part = lax.dot_general(
                WH[w, rows, :],
                N[w, p],
                (((1,), (1,)), ((), ())),
                preferred_element_type=f32,
            )
            total = part if total is None else total + part
        out[rows, :] = total

    logit_in = {}

    def logits_step(s, v):
        rows = pl.ds(SPLIT[v], SPLIT[v + 1] - SPLIT[v])
        for way in (0, 1):
            if s == 4 and v != way:
                continue
            logits_part(POS[s if way == 0 else -s], v, PB.at[way])
        for way in (0, 1):
            if s == 4 and v != way:
                continue
            total = PB[way, rows, :]
            if (way, s + 1, v) in logit_in:
                net.got(logit_in[way, s + 1, v], ER.at[way, s, rows])
                total += ER[way, s, rows, :].astype(f32)
            ES[way, s - 1, rows, :] = total.astype(bf16)
            logit_in[way, s, v] = net.put(
                ES.at[way, s - 1, rows], ER.at[way, s - 1, rows], ring[way]
            )

    def got_head(i):
        net.got(wh_in[i], WH.at[1, pl.ds(PIECES[i], PIECES[i + 1] - PIECES[i])])

    got_head(0)
    got_head(1)
    logits_step(4, 0)
    got_head(2)
    got_head(3)
    logits_step(4, 1)
    logits_step(3, 0)
    logits_step(3, 1)

    for o in range(1, Z):
        net.got(sq_in[o - 1], SQ.at[at_z(-o)])
    total = SQ[0]
    for i in range(1, Z):
        total += SQ[i]
    r = lax.rsqrt(total[0:1] / D + 1e-05)
    CB[...] = jnp.broadcast_to(r, (ROWS, ROWS)).T.reshape(8, 16, ROWS)
    for p in range(8):
        RC[0, p, strip, :] = CB[at_z(DISTANCE[p])]
    rx_in = [
        net.put(RC.at[0, :, strip], RC.at[0, :, strip], x_peer(o)) for o in (1, 2, 3)
    ]
    logits_step(2, 0)
    for o in (1, 2, 3):
        net.got(rx_in[o - 1], RC.at[0, :, lines(c * 64 + x_to(-o) * 16, 16)])
    rc_in = net.put(RC.at[0, :, mine], RC.at[0, :, mine], core_peer)
    ry_in = net.put(RC.at[0, :, mine], RC.at[1, :, mine], y_other)
    logits_step(2, 1)
    net.got(ry_in, RC.at[1, :, mine])
    rf_in = net.put(RC.at[1, :, mine], RC.at[1, :, mine], core_peer)
    logits_step(1, 0)
    net.got(rc_in, RC.at[0, :, others])
    net.got(rf_in, RC.at[1, :, others])
    logits_step(1, 1)

    side = lax.rem(g + yl, 2)
    away = lax.rem(t - z + Z, Z)
    far = lax.div(away, 5)
    p = (1 - far) * (2 * away - 1) + far * (16 - 2 * away) + lax.div(Z - away, Z)
    rows = lines(side * ROWS, ROWS)
    normed_out[...] = (N[0, p, rows, :].astype(f32) * RC[side, p][:, 0:1]).astype(bf16)

    for o in range(1, 16):
        net.got(label_in[o - 1], LA.at[lax.rem(d - o + 16, 16)])
    domain = lax.broadcasted_iota(jnp.int32, (8, ROWS), 0)
    counts = jnp.zeros((8, ROWS), f32)
    for i in range(16):
        counts += jnp.where((LA[i] == domain) & (i < d), 1.0, 0.0)
    onehot = jnp.where(labels[...] == domain, 1.0, 0.0)
    earlier = jnp.where(
        lax.broadcasted_iota(jnp.int32, (ROWS, ROWS), 0)
        < lax.broadcasted_iota(jnp.int32, (ROWS, ROWS), 1),
        1.0,
        0.0,
    )
    before = jnp.dot(
        onehot.astype(bf16), earlier.astype(bf16), preferred_element_type=f32
    ) + jnp.sum(counts, axis=1, keepdims=True)
    rank = jnp.sum(onehot * before, axis=0, keepdims=True)
    allowed = jnp.zeros((1, ROWS), jnp.int32)
    for e in range(8):
        allowed = jnp.where(labels[...] == e, quotas[e], allowed)

    for v in (0, 1):
        logits_part(0, v, PB.at[0])
    net.got(token_in, TK.at[1])
    scale = jnp.concatenate([RC[0, 0].T[0:1], RC[1, 0].T[0:1]], axis=1)
    tokens = jnp.concatenate([TK[0, 0:1], TK[1, 0:1]], axis=1)
    first = (g * 8 + t) * VOC + yl * SHIFT
    for v in (0, 1):
        rows = pl.ds(SPLIT[v], SPLIT[v + 1] - SPLIT[v])
        for way in (0, 1):
            net.got(logit_in[way, 1, v], ER.at[way, 0, rows])

    def summed(k, sums):
        rows = pl.ds(pl.multiple_of(k * 48, 16), 48)
        v = PB[0, rows, :] + ER[0, 0, rows, :].astype(f32)
        v = (v + ER[1, 0, rows, :].astype(f32)) * scale
        row = k * 48 + lax.broadcasted_iota(jnp.int32, (48, 2 * ROWS), 0)
        counted = row >= yl * (2 * MINE - VOC)
        hit = jnp.where(counted & (row + first == tokens), v, 0.0)
        e = jnp.where(counted, jnp.exp(v), 0.0)
        return (
            sums[0] + jnp.sum(e.reshape(6, 8, 2 * ROWS), axis=0),
            sums[1] + jnp.sum(hit.reshape(6, 8, 2 * ROWS), axis=0),
        )

    zero = jnp.zeros((8, 2 * ROWS), f32)
    sums = lax.fori_loop(0, MINE // 48, summed, (zero, zero))
    sumexp, target = (jnp.sum(v, axis=0, keepdims=True) for v in sums)
    wide = lax.broadcasted_iota(jnp.int32, (8, 2 * ROWS), 0)
    pair = jnp.where(wide < 4, sumexp, target)

    FB[0] = pair[:, ROWS:]
    i = net.put(FB.at[0], FR.at[0], y_peer)
    net.got(i, FR.at[0])
    pair = pair[:, :ROWS] + FR[0]
    FB[1] = pair
    i = net.put(FB.at[1], FR.at[1], core_peer)
    net.got(i, FR.at[1])
    pair = pair + FR[1]
    FR[2 + x] = pair
    FB[2] = pair
    pair_in = [net.put(FB.at[2], FR.at[2 + x], x_peer(o)) for o in (1, 2, 3)]
    for o in (1, 2, 3):
        net.got(pair_in[o - 1], FR.at[2 + x_to(-o)])
    pair = (FR[2] + FR[3]) + (FR[4] + FR[5])
    FB[3] = pair
    i = net.put(FB.at[3], FR.at[6], grp_peer)
    net.got(i, FR.at[6])
    pair = pair + FR[6]
    loss = jnp.log(pair[0:1]) - pair[4:5]
    loss_out[...] = jnp.where(rank < allowed.astype(f32), loss, 0.0)
    net.drain()


def on_device(tiers, w_merge, norm_gain, w_head, token_ids, labels, quotas):
    f32, bf16, i32 = jnp.float32, jnp.bfloat16, jnp.int32
    vmem = pl.BlockSpec(memory_space=pltpu.VMEM)
    hbm = pl.BlockSpec(memory_space=pl.ANY)
    normed, loss = pl.pallas_call(
        kernel,
        out_shape=(
            jax.ShapeDtypeStruct((ROWS, COLS), bf16),
            jax.ShapeDtypeStruct((1, ROWS), f32),
        ),
        in_specs=[
            hbm, hbm, vmem, hbm, vmem, vmem, pl.BlockSpec(memory_space=pltpu.SMEM),
        ],
        out_specs=(vmem, vmem),
        scratch_shapes=[
            pltpu.VMEM((8, ROWS, FEAT), bf16),
            pltpu.VMEM((2, FEAT, COLS), bf16),
            pltpu.VMEM((2, 8, COLS), f32),
            pltpu.VMEM((2, 8, ROWS), i32),
            pltpu.VMEM((2, MINE, COLS), bf16),
            pltpu.VMEM((16, 8, ROWS), i32),
            pltpu.VMEM((2, 8, 64, COLS), bf16),
            pltpu.VMEM((2, 8, 64, COLS), bf16),
            pltpu.VMEM((2, 8, ROWS, COLS), f32),
            pltpu.VMEM((3, 2, 8, 16, COLS), bf16),
            pltpu.VMEM((3, 2, 8, 16, COLS), bf16),
            pltpu.VMEM((2, 8, 16, COLS), bf16),
            pltpu.VMEM((2, 8, 16, COLS), bf16),
            pltpu.VMEM((8, 16, 128), f32),
            pltpu.VMEM((Z, 8, ROWS), f32),
            pltpu.VMEM((8, 16, ROWS), f32),
            pltpu.VMEM((2, 8, ROWS, 128), f32),
            pltpu.VMEM((2, 8, 2 * ROWS, COLS), bf16),
            pltpu.VMEM((2, 4, MINE, 2 * ROWS), bf16),
            pltpu.VMEM((2, 4, MINE, 2 * ROWS), bf16),
            pltpu.VMEM((2, MINE, 2 * ROWS), f32),
            pltpu.VMEM((4, 8, ROWS), f32),
            pltpu.VMEM((7, 8, ROWS), f32),
            pltpu.SemaphoreType.DMA((N_SEMS,)),
            pltpu.SemaphoreType.DMA((N_SEMS,)),
            pltpu.SemaphoreType.DMA((3,)),
        ],
        compiler_params=pltpu.CompilerParams(
            collective_id=0, has_side_effects=True, vmem_limit_bytes=56 * 2**20
        ),
    )(
        tiers,
        w_merge,
        norm_gain.reshape(1, COLS),
        w_head.T,
        token_ids.reshape(1, ROWS),
        labels.reshape(1, ROWS),
        quotas,
    )
    return normed, loss.reshape(ROWS)


def solution(mesh):
    both = ("grp", "tp")
    in_specs = (
        P("dp", both),
        P(both, "dp"),
        P("dp"),
        P("dp", both),
        P("dp"),
        P("dp"),
        P(),
    )
    out_specs = (P(both, "dp"), P("dp"))
    return jax.shard_map(
        on_device, mesh=mesh, in_specs=in_specs, out_specs=out_specs, check_vma=False
    )
```

time: 379 us -> 151 us (0.40)
  waiting for transfers between devices: 268 us -> 0 us
  Pallas kernels: 0 us -> 148 us
  blocking collectives: 50.7 us -> 0 us
  matrix products: 15.2 us -> 0 us
  local copies, waits for them, and re-layouts: 16.2 us -> 2.74 us
  between operations: 13.9 us -> 0.64 us
  starting transfers between devices: 10.5 us -> 0 us
  other arithmetic: 3.81 us -> 0 us
    pallas_call x0 -> x1, Pallas kernels: none -> 148 us  [on_device(): pl.pallas_call(kernel, out_shape=(jax.ShapeDtypeStruct((ROWS, COLS), bf16...]
    reduce_scatter x1 -> x0, waiting for transfers between devices: 87.9 us -> none  [on_device(): lax.psum_scatter(partial_value, ('grp', 'tp'), scatter_dimension=0, tiled...]
    all_gather x1 -> x0, waiting for transfers between devices: 84.2 us -> none  [on_device(): lax.all_gather(tiers, 'dp', axis=0, tiled=True)]
    unnamed x4 -> x0, waiting for transfers between devices: 81.7 us -> none
    all_to_all x2 -> x0, blocking collectives: 50.7 us -> none  [sent_to_all(): return lax.all_to_all(copies, axis, split_axis=0, concat_axis=0, tiled=True)]
    dot_general x2 -> x0, matrix products: 15.2 us -> none  [the longest x1 8.68 us: on_device(): jnp.dot(lax.all_gather(tiers, 'dp', axis=0, tiled=True), w_merge, preferr...]
    all_to_all x2 -> x0, waiting for transfers between devices: 13.9 us -> none  [sent_to_all(): return lax.all_to_all(copies, axis, split_axis=0, concat_axis=0, tiled=True)]
    unnamed x14 -> x2, local copies, waits for them, and re-layouts: 14.3 us -> 2.74 us
  transfers between devices with their start and end apart: 5 -> 0, of which waited for: 5 -> 0; matrix products, arithmetic and copies ran while one was open for 1% -> 0% of each run, Pallas kernels for 0% -> 0%
where the time goes in v2:
time: 151 us
  Pallas kernels  148 us (98%)
  local copies, waits for them, and re-layouts  2.74 us (2%)
    pallas_call x1, Pallas kernels, on_device(): pl.pallas_call(kernel, out_shape=(jax.ShapeDtypeStruct((ROWS, COLS), bf16...  148 us

profile of v2, /device:TPU:1, one launch (start us, length us, event | category | flops | bytes accessed | tf_op | source)
XLA Modules:
  0.0 151.3 jit_solution(16104042828455359598)
XLA Ops:
  0.6 147.9 %shard_map.86 = (bf16[128,512]{1,0:T(8,128)(2,1)}, f32[1,128]{1,0:T(1,128)}) custom-call(bf16[128,1536]{1,0:T(8,128)(2,1)} %tiers.1, bf16[1536,512]{1,0:T(8,128)(2,1)} %w_merge.1, f32[1,512]{1,0:T(1,128)} %bitcast.6, bf16[2000,512]{1,0:T(8,128)(2,1)} %bitcast.5, s32[1,128]{1,0:T(1,128)} %bitcast.7, s32[1,128]{1,0:T(1,128)} %bitcast.8, s32[8]{0:T(128)} %quotas.1), custom_call_target="tpu_custom_call" | custom-call | tf_op jit(solution)/shard_map/pallas_call | solution.py:440
  148.5 1.6 %copy.11 = bf16[128,512]{1,0:T(8,128)(2,1)} copy(bf16[128,512]{1,0:T(8,128)(2,1)} %get-tuple-element.8) | data formatting | bytes 262144
  150.1 1.2 copy.12

commit v3 on v2

--- a/solution.py
+++ b/solution.py
@@ -15,7 +15,7 @@
 SHIFT = VOC - MINE
 SPLIT = (0, 528, MINE)
 PIECES = (0, 272, 528, 768, MINE)
-N_SEMS = 140
+N_SEMS = 180
 DISTANCE = (0, 1, -1, 2, -2, 3, -3, 4)
 POS = {s: i for i, s in enumerate(DISTANCE)} | {-4: 7}
 
@@ -89,7 +89,9 @@
         return pl.ds(pl.multiple_of(start, 16), size)
 
     barrier = pltpu.get_barrier_semaphore()
-    peers = [core_peer, grp_peer, y_other]
+    y_core = {"dp": (1 - yl) * Z + z, "tp": 2 * x + 1 - c}
+    peers = [core_peer, grp_peer, y_other, y_core]
+    peers += [{"grp": 1 - g, **x_peer(o)} for o in (1, 2, 3)]
     peers += [x_peer(o) for o in (1, 2, 3)] + [dp_peer(o) for o in range(1, 16)]
     for peer in peers:
         pl.semaphore_signal(
@@ -122,9 +124,19 @@
                 tiers.at[half(h)], T.at[from_way(way, 1), half(h)], ring[way]
             )
     w_in = []
-    for q in (0, 1):
-        cols = pl.ds(256 * q, 256)
-        w_in.append(net.put(w_merge.at[:, cols], W.at[1, :, cols], y_peer))
+
+    def merge_part(i):
+        return pl.ds(768 * (i % 2), 768), pl.ds(128 * (i // 2), 128)
+
+    def merge_piece(i):
+        rows, cols = merge_part(i)
+        w_in.append(net.put(w_merge.at[rows, cols], W.at[1, rows, cols], y_peer))
+
+    def got_merge(i):
+        net.got(w_in[i], W.at[(1, *merge_part(i))])
+
+    merge_piece(0)
+    merge_piece(1)
     gain_in = net.put(G.at[0], G.at[1], y_peer)
     token_in = net.put(TK.at[0], TK.at[1], y_peer)
     label_in = [net.put(LA.at[d], LA.at[d], dp_peer(o)) for o in range(1, 16)]
@@ -140,10 +152,12 @@
 
     batches = {
         "a": (0, 0, 3, 0, COLS),
-        "b": (0, 3, 7, 0, COLS),
-        "c": (0, 7, 8, 0, COLS),
-        "d": (1, 0, 8, 0, 256),
-        "e": (1, 0, 8, 256, COLS),
+        "b": (0, 3, 5, 0, COLS),
+        "c": (1, 0, 5, 0, 256),
+        "d": (0, 5, 7, 0, COLS),
+        "e": (0, 7, 8, 0, COLS),
+        "f": (1, 5, 8, 0, 256),
+        "g": (1, 0, 8, 256, COLS),
     }
     in1, in2, in3, inx, inc, iny, inf = {}, {}, {}, {}, {}, {}, {}
     mine, others = lines(c * 64, 64), lines((1 - c) * 64, 64)
@@ -225,59 +239,77 @@
         wh_in.append(net.put(w_head.at[rows], to, y_peer))
 
     ring_step(1, 0)
+    merge_piece(2)
     ring_step(1, 1)
+    merge_piece(3)
     keep_local[0].wait()
     keep_local[1].wait()
     stage1("a")
     ring_step(2, 0)
+    merge_piece(4)
     stage2("a")
     ring_step(2, 1)
+    merge_piece(5)
+    stage1("b")
     stage3("a")
     ring_step(3, 0)
+    merge_piece(6)
+    net.got(gain_in, G.at[1])
+    for i in range(4):
+        got_merge(i)
+    stage1("c")
+    stage2("b")
+    ring_step(3, 1)
+    merge_piece(7)
+    stage1("d")
     stage4("a")
-    ring_step(3, 1)
-    stage1("b")
-    spread("a")
+    stage2("c")
+    stage3("b")
     ring_step(4, 0)
     ring_step(4, 1)
-    stage1("c")
-    stage2("b")
-    net.got(w_in[0], W.at[1, :, pl.ds(0, 256)])
-    stage1("d")
-    stage2("c")
-    stage3("b")
-    net.got(w_in[1], W.at[1, :, pl.ds(256, 256)])
     stage1("e")
-    net.sent(w_in)
-    head_piece(0)
+    stage1("f")
     stage2("d")
     stage3("c")
-    net.got(gain_in, G.at[1])
+    spread("a")
+    for i in range(4, 8):
+        got_merge(i)
+    stage1("g")
+    head_piece(0)
     stage4("b")
     stage2("e")
+    stage2("f")
     stage3("d")
     stage4("c")
-    head_piece(1)
-    spread2("a")
+    stage2("g")
     spread("b")
     stage3("e")
+    stage3("f")
     stage4("d")
+    head_piece(1)
     spread("c")
+    stage3("g")
+    spread2("a")
     stage4("e")
-    head_piece(2)
+    stage4("f")
     spread2("b")
     spread("d")
+    stage4("g")
+    head_piece(2)
     spread2("c")
+    spread("e")
+    spread("f")
+    spread2("d")
 
     by_row = SA[...].reshape(ROWS, 128).T
     SQ[z] = jnp.broadcast_to(jnp.sum(by_row, axis=0, keepdims=True), (8, ROWS))
     sq_in = [
         net.put(SQ.at[z], SQ.at[z], {"dp": yl * Z + at_z(o)}) for o in range(1, Z)
     ]
-    spread("e")
+    spread("g")
     head_piece(3)
-    spread2("d")
-    spread2("e")
+    for k in ("e", "f", "g"):
+        spread2(k)
     keep_local[2].wait()
     for k in batches:
         spread3(k)
@@ -297,15 +329,11 @@
 
     logit_in = {}
 
-    def logits_step(s, v):
-        rows = pl.ds(SPLIT[v], SPLIT[v + 1] - SPLIT[v])
-        for way in (0, 1):
-            if s == 4 and v != way:
-                continue
+    def logits_step(*parts):
+        for s, v, way in parts:
             logits_part(POS[s if way == 0 else -s], v, PB.at[way])
-        for way in (0, 1):
-            if s == 4 and v != way:
-                continue
+        for s, v, way in parts:
+            rows = pl.ds(SPLIT[v], SPLIT[v + 1] - SPLIT[v])
             total = PB[way, rows, :]
             if (way, s + 1, v) in logit_in:
                 net.got(logit_in[way, s + 1, v], ER.at[way, s, rows])
@@ -320,12 +348,12 @@
 
     got_head(0)
     got_head(1)
-    logits_step(4, 0)
+    logits_step((4, 0, 0), (3, 0, 1))
     got_head(2)
     got_head(3)
-    logits_step(4, 1)
-    logits_step(3, 0)
-    logits_step(3, 1)
+    logits_step((3, 1, 0), (4, 1, 1))
+    logits_step((3, 0, 0), (2, 0, 1))
+    logits_step((2, 1, 0), (3, 1, 1))
 
     for o in range(1, Z):
         net.got(sq_in[o - 1], SQ.at[at_z(-o)])
@@ -339,18 +367,18 @@
     rx_in = [
         net.put(RC.at[0, :, strip], RC.at[0, :, strip], x_peer(o)) for o in (1, 2, 3)
     ]
-    logits_step(2, 0)
+    logits_step((2, 0, 0), (1, 0, 1))
     for o in (1, 2, 3):
         net.got(rx_in[o - 1], RC.at[0, :, lines(c * 64 + x_to(-o) * 16, 16)])
     rc_in = net.put(RC.at[0, :, mine], RC.at[0, :, mine], core_peer)
     ry_in = net.put(RC.at[0, :, mine], RC.at[1, :, mine], y_other)
-    logits_step(2, 1)
+    logits_step((1, 1, 0), (2, 1, 1))
     net.got(ry_in, RC.at[1, :, mine])
     rf_in = net.put(RC.at[1, :, mine], RC.at[1, :, mine], core_peer)
-    logits_step(1, 0)
+    logits_step((1, 0, 0))
     net.got(rc_in, RC.at[0, :, others])
     net.got(rf_in, RC.at[1, :, others])
-    logits_step(1, 1)
+    logits_step((1, 1, 1))
 
     side = lax.rem(g + yl, 2)
     away = lax.rem(t - z + Z, Z)
@@ -410,24 +438,31 @@
     wide = lax.broadcasted_iota(jnp.int32, (8, 2 * ROWS), 0)
     pair = jnp.where(wide < 4, sumexp, target)
 
-    FB[0] = pair[:, ROWS:]
-    i = net.put(FB.at[0], FR.at[0], y_peer)
-    net.got(i, FR.at[0])
-    pair = pair[:, :ROWS] + FR[0]
-    FB[1] = pair
-    i = net.put(FB.at[1], FR.at[1], core_peer)
-    net.got(i, FR.at[1])
-    pair = pair + FR[1]
-    FR[2 + x] = pair
+    FR[c] = pair[:, :ROWS]
+    FB[0] = pair[:, :ROWS]
+    FB[1] = pair[:, ROWS:]
+    near = [
+        net.put(FB.at[0], FR.at[c], core_peer),
+        net.put(FB.at[1], FR.at[2 + c], y_peer),
+        net.put(FB.at[1], FR.at[2 + c], y_core),
+    ]
+    net.got(near[0], FR.at[1 - c])
+    net.got(near[1], FR.at[2 + c])
+    net.got(near[2], FR.at[3 - c])
+    pair = (FR[0] + FR[1]) + (FR[2] + FR[3])
+    at = 4 + 4 * g
     FB[2] = pair
-    pair_in = [net.put(FB.at[2], FR.at[2 + x], x_peer(o)) for o in (1, 2, 3)]
-    for o in (1, 2, 3):
-        net.got(pair_in[o - 1], FR.at[2 + x_to(-o)])
-    pair = (FR[2] + FR[3]) + (FR[4] + FR[5])
-    FB[3] = pair
-    i = net.put(FB.at[3], FR.at[6], grp_peer)
-    net.got(i, FR.at[6])
-    pair = pair + FR[6]
+    FR[at + x] = pair
+    across = [
+        (net.put(FB.at[2], FR.at[at + x], {"grp": g if same else 1 - g, **x_peer(o)}), same, o)
+        for same in (True, False)
+        for o in range(4)
+        if o or not same
+    ]
+    for handle, same, o in across:
+        net.got(handle, FR.at[(at if same else 8 - 4 * g) + x_to(-o)])
+    pair = (FR[4] + FR[5]) + (FR[6] + FR[7])
+    pair += (FR[8] + FR[9]) + (FR[10] + FR[11])
     loss = jnp.log(pair[0:1]) - pair[4:5]
     loss_out[...] = jnp.where(rank < allowed.astype(f32), loss, 0.0)
     net.drain()
@@ -469,8 +504,8 @@
             pltpu.VMEM((2, 4, MINE, 2 * ROWS), bf16),
             pltpu.VMEM((2, 4, MINE, 2 * ROWS), bf16),
             pltpu.VMEM((2, MINE, 2 * ROWS), f32),
-            pltpu.VMEM((4, 8, ROWS), f32),
-            pltpu.VMEM((7, 8, ROWS), f32),
+            pltpu.VMEM((3, 8, ROWS), f32),
+            pltpu.VMEM((12, 8, ROWS), f32),
             pltpu.SemaphoreType.DMA((N_SEMS,)),
             pltpu.SemaphoreType.DMA((N_SEMS,)),
             pltpu.SemaphoreType.DMA((3,)),

time: 151 us -> 139 us (0.921)
  Pallas kernels: 148 us -> 135 us
    pallas_call x1, Pallas kernels: 148 us -> 135 us  [on_device(): pl.pallas_call(kernel, out_shape=(jax.ShapeDtypeStruct((ROWS, COLS), bf16...]
where the time goes in v3:
time: 139 us; the launch traced here: 138 us
  Pallas kernels  135 us (97%)
  local copies, waits for them, and re-layouts  2.74 us (2%)
    pallas_call x1, Pallas kernels, on_device(): pl.pallas_call(kernel, out_shape=(jax.ShapeDtypeStruct((ROWS, COLS), bf16...  135 us

profile of v3, /device:TPU:1, one launch (start us, length us, event | category | flops | bytes accessed | tf_op | source)
XLA Modules:
  0.0 138.4 jit_solution(18201341814706463370)
XLA Ops:
  0.6 135.0 %shard_map.86 = (bf16[128,512]{1,0:T(8,128)(2,1)}, f32[1,128]{1,0:T(1,128)}) custom-call(bf16[128,1536]{1,0:T(8,128)(2,1)} %tiers.1, bf16[1536,512]{1,0:T(8,128)(2,1)} %w_merge.1, f32[1,512]{1,0:T(1,128)} %bitcast.6, bf16[2000,512]{1,0:T(8,128)(2,1)} %bitcast.5, s32[1,128]{1,0:T(1,128)} %bitcast.7, s32[1,128]{1,0:T(1,128)} %bitcast.8, s32[8]{0:T(128)} %quotas.1), custom_call_target="tpu_custom_call" | custom-call | tf_op jit(solution)/shard_map/pallas_call | solution.py:475
  135.6 1.6 %copy.11 = bf16[128,512]{1,0:T(8,128)(2,1)} copy(bf16[128,512]{1,0:T(8,128)(2,1)} %get-tuple-element.8) | data formatting | bytes 262144
  137.2 1.2 copy.12

commit v4 on v3

--- a/solution.py
+++ b/solution.py
@@ -15,7 +15,7 @@
 SHIFT = VOC - MINE
 SPLIT = (0, 528, MINE)
 PIECES = (0, 272, 528, 768, MINE)
-N_SEMS = 180
+N_SEMS = 200
 DISTANCE = (0, 1, -1, 2, -2, 3, -3, 4)
 POS = {s: i for i, s in enumerate(DISTANCE)} | {-4: 7}
 
@@ -37,6 +37,7 @@
     def put(self, src, dst, device):
         i = self.n
         self.n += 1
+        assert i < N_SEMS
         copy = self.make(src, dst, device, i)
         copy.start()
         self.started[i] = copy
@@ -82,9 +83,6 @@
     def x_peer(o):
         return {"tp": 2 * x_to(o) + c}
 
-    def dp_peer(o):
-        return {"dp": lax.rem(d + o, 16)}
-
     def lines(start, size):
         return pl.ds(pl.multiple_of(start, 16), size)
 
@@ -92,7 +90,7 @@
     y_core = {"dp": (1 - yl) * Z + z, "tp": 2 * x + 1 - c}
     peers = [core_peer, grp_peer, y_other, y_core]
     peers += [{"grp": 1 - g, **x_peer(o)} for o in (1, 2, 3)]
-    peers += [x_peer(o) for o in (1, 2, 3)] + [dp_peer(o) for o in range(1, 16)]
+    peers += [x_peer(o) for o in (1, 2, 3)] + [*ring, y_peer]
     for peer in peers:
         pl.semaphore_signal(
             barrier, inc=1, device_id=peer, device_id_type=pl.DeviceIdType.MESH
@@ -135,11 +133,18 @@
     def got_merge(i):
         net.got(w_in[i], W.at[(1, *merge_part(i))])
 
-    merge_piece(0)
-    merge_piece(1)
+    for i in range(3):
+        merge_piece(i)
     gain_in = net.put(G.at[0], G.at[1], y_peer)
     token_in = net.put(TK.at[0], TK.at[1], y_peer)
-    label_in = [net.put(LA.at[d], LA.at[d], dp_peer(o)) for o in range(1, 16)]
+    label_in = {(way, 1): net.put(LA.at[d], LA.at[d], ring[way]) for way in (0, 1)}
+
+    def small_step(buf, first, handles, way, s):
+        if (way, s) in handles:
+            piece = buf.at[first + at_z(-s if way == 0 else s)]
+            net.got(handles[way, s], piece)
+            if s < 3 or (s == 3 and way == 0):
+                handles[way, s + 1] = net.put(piece, piece, ring[way])
 
     def ring_step(s, h):
         for way in (0, 1):
@@ -149,6 +154,7 @@
                 if s < 3 or (s == 3 and h == way):
                     to = T.at[from_way(way, s + 1), half(h)]
                     tier_in[way, s + 1, h] = net.put(piece, to, ring[way])
+        small_step(LA, yl * Z, label_in, h, s)
 
     batches = {
         "a": (0, 0, 3, 0, COLS),
@@ -156,8 +162,11 @@
         "c": (1, 0, 5, 0, 256),
         "d": (0, 5, 7, 0, COLS),
         "e": (0, 7, 8, 0, COLS),
-        "f": (1, 5, 8, 0, 256),
-        "g": (1, 0, 8, 256, COLS),
+        "f": (1, 5, 7, 0, 256),
+        "g": (1, 0, 7, 256, 384),
+        "h": (1, 7, 8, 0, 384),
+        "i": (1, 0, 8, 384, COLS),
+        "ab": (0, 0, 5, 0, COLS),
     }
     in1, in2, in3, inx, inc, iny, inf = {}, {}, {}, {}, {}, {}, {}
     mine, others = lines(c * 64, 64), lines((1 - c) * 64, 64)
@@ -209,27 +218,43 @@
         for o in (1, 2, 3):
             inx[k, o] = net.put(piece, piece, x_peer(o))
 
-    def rows_of(k, rows, other_w=False):
-        w, p0, p1, c0, c1 = batches[k]
-        w = 1 - w if other_w else w
-        return N.at[w, pl.ds(p0, p1 - p0), rows, pl.ds(c0, c1 - c0)]
-
     there, there_others = lines(ROWS + c * 64, 64), lines(ROWS + (1 - c) * 64, 64)
 
-    def spread(k):
-        for o in (1, 2, 3):
-            net.got(inx[k, o], rows_of(k, lines(c * 64 + x_to(-o) * 16, 16)))
-        inc[k] = net.put(rows_of(k, mine), rows_of(k, mine), core_peer)
-        iny[k] = net.put(rows_of(k, mine), rows_of(k, there, True), y_other)
-
-    def spread2(k):
-        net.got(iny[k], rows_of(k, there, True))
-        piece = rows_of(k, there, True)
-        inf[k] = net.put(piece, piece, core_peer)
-
-    def spread3(k):
-        net.got(inc[k], rows_of(k, others))
-        net.got(inf[k], rows_of(k, there_others, True))
+    def spread(*keys):
+        for k in keys:
+            w, p0, p1, c0, c1 = batches[k]
+            blocks, cols = pl.ds(p0, p1 - p0), pl.ds(c0, c1 - c0)
+            for o in (1, 2, 3):
+                rows = lines(c * 64 + x_to(-o) * 16, 16)
+                net.got(inx[k, o], N.at[w, blocks, rows, cols])
+            piece = N.at[w, blocks, mine, cols]
+            inc[k] = net.put(piece, piece, core_peer)
+
+    def have_near():
+        for k, handle in inc.items():
+            w, p0, p1, c0, c1 = batches[k]
+            net.got(handle, N.at[w, pl.ds(p0, p1 - p0), others, pl.ds(c0, c1 - c0)])
+
+    def to_far(*keys):
+        for k in keys:
+            w, p0, p1, c0, c1 = batches[k]
+            blocks, cols = pl.ds(p0, p1 - p0), pl.ds(c0, c1 - c0)
+            iny[k] = net.put(
+                N.at[w, blocks, mine, cols], N.at[1 - w, blocks, there, cols], y_other
+            )
+
+    def pass_far(*keys):
+        for k in keys:
+            w, p0, p1, c0, c1 = batches[k]
+            piece = N.at[1 - w, pl.ds(p0, p1 - p0), there, pl.ds(c0, c1 - c0)]
+            net.got(iny[k], piece)
+            inf[k] = net.put(piece, piece, core_peer)
+
+    def have_far():
+        for k, handle in inf.items():
+            w, p0, p1, c0, c1 = batches[k]
+            blocks, cols = pl.ds(p0, p1 - p0), pl.ds(c0, c1 - c0)
+            net.got(handle, N.at[1 - w, blocks, there_others, cols])
 
     wh_in = []
 
@@ -239,108 +264,112 @@
         wh_in.append(net.put(w_head.at[rows], to, y_peer))
 
     ring_step(1, 0)
-    merge_piece(2)
+    merge_piece(3)
     ring_step(1, 1)
-    merge_piece(3)
+    merge_piece(4)
     keep_local[0].wait()
     keep_local[1].wait()
     stage1("a")
+    stage2("a")
     ring_step(2, 0)
-    merge_piece(4)
-    stage2("a")
+    merge_piece(5)
+    stage3("a")
     ring_step(2, 1)
-    merge_piece(5)
+    merge_piece(6)
     stage1("b")
-    stage3("a")
     ring_step(3, 0)
-    merge_piece(6)
+    merge_piece(7)
+    stage2("b")
     net.got(gain_in, G.at[1])
     for i in range(4):
         got_merge(i)
     stage1("c")
-    stage2("b")
     ring_step(3, 1)
-    merge_piece(7)
     stage1("d")
-    stage4("a")
+    stage1("f")
+    got_merge(4)
+    got_merge(5)
+    stage1("g")
     stage2("c")
     stage3("b")
+    stage4("a")
+    for k in ("d", "f", "g"):
+        stage2(k)
     ring_step(4, 0)
     ring_step(4, 1)
     stage1("e")
-    stage1("f")
-    stage2("d")
+    stage1("h")
     stage3("c")
+    got_merge(6)
+    got_merge(7)
+    stage1("i")
+    head_piece(0)
+    stage2("e")
+    stage2("h")
+    for k in ("d", "f", "g"):
+        stage3(k)
+    stage2("i")
+    stage4("b")
     spread("a")
-    for i in range(4, 8):
-        got_merge(i)
-    stage1("g")
-    head_piece(0)
-    stage4("b")
-    stage2("e")
-    stage2("f")
-    stage3("d")
     stage4("c")
-    stage2("g")
+    stage3("e")
+    stage3("h")
+    for k in ("d", "f", "g"):
+        stage4(k)
+    stage3("i")
+    head_piece(1)
+    stage4("e")
+    stage4("h")
     spread("b")
-    stage3("e")
-    stage3("f")
-    stage4("d")
-    head_piece(1)
     spread("c")
-    stage3("g")
-    spread2("a")
-    stage4("e")
-    stage4("f")
-    spread2("b")
-    spread("d")
-    stage4("g")
+    to_far("ab", "c")
+    spread("d", "f", "g")
+    to_far("d", "f", "g")
+    stage4("i")
     head_piece(2)
-    spread2("c")
-    spread("e")
-    spread("f")
-    spread2("d")
+    head_piece(3)
 
     by_row = SA[...].reshape(ROWS, 128).T
     SQ[z] = jnp.broadcast_to(jnp.sum(by_row, axis=0, keepdims=True), (8, ROWS))
-    sq_in = [
-        net.put(SQ.at[z], SQ.at[z], {"dp": yl * Z + at_z(o)}) for o in range(1, Z)
-    ]
-    spread("g")
-    head_piece(3)
-    for k in ("e", "f", "g"):
-        spread2(k)
+    square_in = {(way, 1): net.put(SQ.at[z], SQ.at[z], ring[way]) for way in (0, 1)}
+    spread("e", "h", "i")
+    to_far("e", "h", "i")
+    half_labels = LA.at[pl.ds(yl * Z, Z)]
+    y_labels = net.put(half_labels, half_labels, y_peer)
     keep_local[2].wait()
-    for k in batches:
-        spread3(k)
-
-    def logits_part(p, v, out):
+    have_near()
+
+    def piece_of(v, far):
         rows = pl.ds(SPLIT[v], SPLIT[v + 1] - SPLIT[v])
+        return rows, pl.ds(ROWS * far, ROWS)
+
+    def logits_part(p, v, far, out):
+        rows, lanes = piece_of(v, far)
         total = None
         for w in (0, 1):
             part = lax.dot_general(
                 WH[w, rows, :],
-                N[w, p],
+                N[w, p, lanes, :],
                 (((1,), (1,)), ((), ())),
                 preferred_element_type=f32,
             )
             total = part if total is None else total + part
-        out[rows, :] = total
+        out[rows, lanes] = total
 
     logit_in = {}
 
     def logits_step(*parts):
-        for s, v, way in parts:
-            logits_part(POS[s if way == 0 else -s], v, PB.at[way])
-        for s, v, way in parts:
-            rows = pl.ds(SPLIT[v], SPLIT[v + 1] - SPLIT[v])
-            total = PB[way, rows, :]
-            if (way, s + 1, v) in logit_in:
-                net.got(logit_in[way, s + 1, v], ER.at[way, s, rows])
-                total += ER[way, s, rows, :].astype(f32)
-            ES[way, s - 1, rows, :] = total.astype(bf16)
-            logit_in[way, s, v] = net.put(
-                ES.at[way, s - 1, rows], ER.at[way, s - 1, rows], ring[way]
+        for way, (s, v, far) in enumerate(parts):
+            logits_part(POS[s if way == 0 else -s], v, far, PB.at[way])
+        for way, (s, v, far) in enumerate(parts):
+            at = piece_of(v, far)
+            total = PB[(way, *at)]
+            if (way, s + 1, v, far) in logit_in:
+                net.got(logit_in[way, s + 1, v, far], ER.at[(way, s, *at)])
+                total += ER[(way, s, *at)].astype(f32)
+            ES[(way, s - 1, *at)] = total.astype(bf16)
+            logit_in[way, s, v, far] = net.put(
+                ES.at[(way, s - 1, *at)], ER.at[(way, s - 1, *at)], ring[way]
             )
 
     def got_head(i):
@@ -348,15 +377,30 @@
 
     got_head(0)
     got_head(1)
-    logits_step((4, 0, 0), (3, 0, 1))
+    def squares_step(s):
+        for way in (0, 1):
+            small_step(SQ, 0, square_in, way, s)
+
+    logits_step((4, 0, 0), (3, 0, 0))
+    logits_step((3, 0, 0), (2, 0, 0))
+    squares_step(1)
+    pass_far("ab", "c")
     got_head(2)
     got_head(3)
-    logits_step((3, 1, 0), (4, 1, 1))
-    logits_step((3, 0, 0), (2, 0, 1))
-    logits_step((2, 1, 0), (3, 1, 1))
-
-    for o in range(1, Z):
-        net.got(sq_in[o - 1], SQ.at[at_z(-o)])
+    logits_step((3, 1, 0), (4, 1, 0))
+    pass_far("d")
+    logits_step((2, 0, 0), (1, 0, 0))
+    squares_step(2)
+    pass_far("f", "g")
+    logits_step((2, 1, 0), (3, 1, 0))
+    pass_far("e", "h", "i")
+    have_far()
+    logits_step((4, 0, 1), (4, 1, 1))
+    squares_step(3)
+    logits_step((1, 0, 0), (2, 1, 0))
+    logits_step((1, 1, 0), (3, 0, 1))
+    squares_step(4)
+
     total = SQ[0]
     for i in range(1, Z):
         total += SQ[i]
@@ -367,18 +411,20 @@
     rx_in = [
         net.put(RC.at[0, :, strip], RC.at[0, :, strip], x_peer(o)) for o in (1, 2, 3)
     ]
-    logits_step((2, 0, 0), (1, 0, 1))
+    logits_step((3, 1, 1), (1, 1, 0))
+    logits_step((3, 0, 1), (3, 1, 1))
     for o in (1, 2, 3):
         net.got(rx_in[o - 1], RC.at[0, :, lines(c * 64 + x_to(-o) * 16, 16)])
     rc_in = net.put(RC.at[0, :, mine], RC.at[0, :, mine], core_peer)
     ry_in = net.put(RC.at[0, :, mine], RC.at[1, :, mine], y_other)
-    logits_step((1, 1, 0), (2, 1, 1))
+    logits_step((2, 1, 1), (2, 0, 1))
+    logits_step((2, 0, 1), (2, 1, 1))
     net.got(ry_in, RC.at[1, :, mine])
     rf_in = net.put(RC.at[1, :, mine], RC.at[1, :, mine], core_peer)
-    logits_step((1, 0, 0))
+    logits_step((1, 1, 1), (1, 0, 1))
+    logits_step((1, 0, 1), (1, 1, 1))
     net.got(rc_in, RC.at[0, :, others])
     net.got(rf_in, RC.at[1, :, others])
-    logits_step((1, 1, 1))
 
     side = lax.rem(g + yl, 2)
     away = lax.rem(t - z + Z, Z)
@@ -387,8 +433,7 @@
     rows = lines(side * ROWS, ROWS)
     normed_out[...] = (N[0, p, rows, :].astype(f32) * RC[side, p][:, 0:1]).astype(bf16)
 
-    for o in range(1, 16):
-        net.got(label_in[o - 1], LA.at[lax.rem(d - o + 16, 16)])
+    net.got(y_labels, LA.at[pl.ds((1 - yl) * Z, Z)])
     domain = lax.broadcasted_iota(jnp.int32, (8, ROWS), 0)
     counts = jnp.zeros((8, ROWS), f32)
     for i in range(16):
@@ -409,38 +454,46 @@
         allowed = jnp.where(labels[...] == e, quotas[e], allowed)
 
     for v in (0, 1):
-        logits_part(0, v, PB.at[0])
+        for far in (0, 1):
+            logits_part(0, v, far, PB.at[0])
     net.got(token_in, TK.at[1])
-    scale = jnp.concatenate([RC[0, 0].T[0:1], RC[1, 0].T[0:1]], axis=1)
-    tokens = jnp.concatenate([TK[0, 0:1], TK[1, 0:1]], axis=1)
+    scale = [RC[far, 0].T[0:1] for far in (0, 1)]
     first = (g * 8 + t) * VOC + yl * SHIFT
-    for v in (0, 1):
-        rows = pl.ds(SPLIT[v], SPLIT[v + 1] - SPLIT[v])
+    def sums_of(v, far):
         for way in (0, 1):
-            net.got(logit_in[way, 1, v], ER.at[way, 0, rows])
-
-    def summed(k, sums):
-        rows = pl.ds(pl.multiple_of(k * 48, 16), 48)
-        v = PB[0, rows, :] + ER[0, 0, rows, :].astype(f32)
-        v = (v + ER[1, 0, rows, :].astype(f32)) * scale
-        row = k * 48 + lax.broadcasted_iota(jnp.int32, (48, 2 * ROWS), 0)
-        counted = row >= yl * (2 * MINE - VOC)
-        hit = jnp.where(counted & (row + first == tokens), v, 0.0)
-        e = jnp.where(counted, jnp.exp(v), 0.0)
-        return (
-            sums[0] + jnp.sum(e.reshape(6, 8, 2 * ROWS), axis=0),
-            sums[1] + jnp.sum(hit.reshape(6, 8, 2 * ROWS), axis=0),
+            net.got(logit_in[way, 1, v, far], ER.at[(way, 0, *piece_of(v, far))])
+        lanes = pl.ds(ROWS * far, ROWS)
+        valid = yl * (2 * MINE - VOC)
+
+        def summed(k, sums):
+            start = SPLIT[v] + k * 48
+            rows = pl.ds(pl.multiple_of(start, 16), 48)
+            u = PB[0, rows, lanes] + ER[0, 0, rows, lanes].astype(f32)
+            u = (u + ER[1, 0, rows, lanes].astype(f32)) * scale[far]
+            row = start + lax.broadcasted_iota(jnp.int32, (48, ROWS), 0)
+            counted = row >= valid
+            hit = jnp.where(counted & (row + first == TK[far, 0:1]), u, 0.0)
+            e = jnp.where(counted, jnp.exp(u), 0.0)
+            return (
+                sums[0] + jnp.sum(e.reshape(6, 8, ROWS), axis=0),
+                sums[1] + jnp.sum(hit.reshape(6, 8, ROWS), axis=0),
+            )
+
+        zero = jnp.zeros((8, ROWS), f32)
+        return lax.fori_loop(0, (SPLIT[v + 1] - SPLIT[v]) // 48, summed, (zero, zero))
+
+    parts = {at: sums_of(*at) for at in ((1, 0), (0, 0), (0, 1), (1, 1))}
+    pairs = []
+    for far in (0, 1):
+        sumexp, target = (
+            jnp.sum(parts[0, far][i] + parts[1, far][i], axis=0, keepdims=True)
+            for i in (0, 1)
         )
-
-    zero = jnp.zeros((8, 2 * ROWS), f32)
-    sums = lax.fori_loop(0, MINE // 48, summed, (zero, zero))
-    sumexp, target = (jnp.sum(v, axis=0, keepdims=True) for v in sums)
-    wide = lax.broadcasted_iota(jnp.int32, (8, 2 * ROWS), 0)
-    pair = jnp.where(wide < 4, sumexp, target)
-
-    FR[c] = pair[:, :ROWS]
-    FB[0] = pair[:, :ROWS]
-    FB[1] = pair[:, ROWS:]
+        pairs.append(jnp.where(domain < 4, sumexp, target))
+
+    FR[c] = pairs[0]
+    FB[0] = pairs[0]
+    FB[1] = pairs[1]
     near = [
         net.put(FB.at[0], FR.at[c], core_peer),
         net.put(FB.at[1], FR.at[2 + c], y_peer),

time: 139 us -> 130 us (0.935)
  Pallas kernels: 135 us -> 127 us
    pallas_call x1, Pallas kernels: 135 us -> 127 us  [on_device(): pl.pallas_call(kernel, out_shape=(jax.ShapeDtypeStruct((ROWS, COLS), bf16...]
where the time goes in v4:
time: 130 us
  Pallas kernels  127 us (98%)
  local copies, waits for them, and re-layouts  2.74 us (2%)
    pallas_call x1, Pallas kernels, on_device(): pl.pallas_call(kernel, out_shape=(jax.ShapeDtypeStruct((ROWS, COLS), bf16...  127 us
    unnamed x2, local copies, waits for them, and re-layouts  2.74 us

profile of v4, /device:TPU:1, one launch (start us, length us, event | category | flops | bytes accessed | tf_op | source)
XLA Modules:
  0.0 130.3 jit_solution(13119949183562868650)
XLA Ops:
  0.6 126.9 %shard_map.86 = (bf16[128,512]{1,0:T(8,128)(2,1)}, f32[1,128]{1,0:T(1,128)}) custom-call(bf16[128,1536]{1,0:T(8,128)(2,1)} %tiers.1, bf16[1536,512]{1,0:T(8,128)(2,1)} %w_merge.1, f32[1,512]{1,0:T(1,128)} %bitcast.6, bf16[2000,512]{1,0:T(8,128)(2,1)} %bitcast.5, s32[1,128]{1,0:T(1,128)} %bitcast.7, s32[1,128]{1,0:T(1,128)} %bitcast.8, s32[8]{0:T(128)} %quotas.1), custom_call_target="tpu_custom_call" | custom-call | tf_op jit(solution)/shard_map/pallas_call | solution.py:528
  127.5 1.6 %copy.11 = bf16[128,512]{1,0:T(8,128)(2,1)} copy(bf16[128,512]{1,0:T(8,128)(2,1)} %get-tuple-element.8) | data formatting | bytes 262144
  129.1 1.2 copy.12

commit v5 on v4

--- a/solution.py
+++ b/solution.py
@@ -14,7 +14,7 @@
 MINE = 1008
 SHIFT = VOC - MINE
 SPLIT = (0, 528, MINE)
-PIECES = (0, 272, 528, 768, MINE)
+PIECES = (0, 144, 528, 768, MINE)
 N_SEMS = 200
 DISTANCE = (0, 1, -1, 2, -2, 3, -3, 4)
 POS = {s: i for i, s in enumerate(DISTANCE)} | {-4: 7}

time: 130 us -> 129 us (level)
    pallas_call x1, Pallas kernels: 127 us -> 126 us  [on_device(): pl.pallas_call(kernel, out_shape=(jax.ShapeDtypeStruct((ROWS, COLS), bf16...]
where the time goes in v5:
time: 129 us
  Pallas kernels  126 us (98%)
  local copies, waits for them, and re-layouts  2.74 us (2%)
    pallas_call x1, Pallas kernels, on_device(): pl.pallas_call(kernel, out_shape=(jax.ShapeDtypeStruct((ROWS, COLS), bf16...  126 us
    unnamed x2, local copies, waits for them, and re-layouts  2.74 us

profile of v5, /device:TPU:1, one launch (start us, length us, event | category | flops | bytes accessed | tf_op | source)
XLA Modules:
  0.0 128.9 jit_solution(9327216639554127274)
XLA Ops:
  0.6 125.5 %shard_map.86 = (bf16[128,512]{1,0:T(8,128)(2,1)}, f32[1,128]{1,0:T(1,128)}) custom-call(bf16[128,1536]{1,0:T(8,128)(2,1)} %tiers.1, bf16[1536,512]{1,0:T(8,128)(2,1)} %w_merge.1, f32[1,512]{1,0:T(1,128)} %bitcast.6, bf16[2000,512]{1,0:T(8,128)(2,1)} %bitcast.5, s32[1,128]{1,0:T(1,128)} %bitcast.7, s32[1,128]{1,0:T(1,128)} %bitcast.8, s32[8]{0:T(128)} %quotas.1), custom_call_target="tpu_custom_call" | custom-call | tf_op jit(solution)/shard_map/pallas_call | solution.py:528
  126.2 1.6 %copy.11 = bf16[128,512]{1,0:T(8,128)(2,1)} copy(bf16[128,512]{1,0:T(8,128)(2,1)} %get-tuple-element.8) | data formatting | bytes 262144
  127.7 1.2 copy.12

commit v6 on v5

--- a/solution.py
+++ b/solution.py
@@ -329,14 +329,15 @@
     head_piece(2)
     head_piece(3)
 
-    by_row = SA[...].reshape(ROWS, 128).T
-    SQ[z] = jnp.broadcast_to(jnp.sum(by_row, axis=0, keepdims=True), (8, ROWS))
-    square_in = {(way, 1): net.put(SQ.at[z], SQ.at[z], ring[way]) for way in (0, 1)}
     spread("e", "h", "i")
     to_far("e", "h", "i")
     half_labels = LA.at[pl.ds(yl * Z, Z)]
     y_labels = net.put(half_labels, half_labels, y_peer)
     keep_local[2].wait()
+
+    by_row = SA[...].reshape(ROWS, 128).T
+    SQ[z] = jnp.broadcast_to(jnp.sum(by_row, axis=0, keepdims=True), (8, ROWS))
+    square_in = {(way, 1): net.put(SQ.at[z], SQ.at[z], ring[way]) for way in (0, 1)}
     have_near()
 
     def piece_of(v, far):

time: 129 us -> 129 us (level)
  no operation moved by 1% of the time
where the time goes in v6:
time: 129 us
  Pallas kernels  126 us (98%)
  local copies, waits for them, and re-layouts  2.74 us (2%)
    pallas_call x1, Pallas kernels, on_device(): pl.pallas_call(kernel, out_shape=(jax.ShapeDtypeStruct((ROWS, COLS), bf16...  126 us
    unnamed x2, local copies, waits for them, and re-layouts  2.74 us

profile of v6, /device:TPU:1, one launch (start us, length us, event | category | flops | bytes accessed | tf_op | source)
XLA Modules:
  0.0 128.9 jit_solution(8846784600663159744)
XLA Ops:
  0.6 125.5 %shard_map.86 = (bf16[128,512]{1,0:T(8,128)(2,1)}, f32[1,128]{1,0:T(1,128)}) custom-call(bf16[128,1536]{1,0:T(8,128)(2,1)} %tiers.1, bf16[1536,512]{1,0:T(8,128)(2,1)} %w_merge.1, f32[1,512]{1,0:T(1,128)} %bitcast.6, bf16[2000,512]{1,0:T(8,128)(2,1)} %bitcast.5, s32[1,128]{1,0:T(1,128)} %bitcast.7, s32[1,128]{1,0:T(1,128)} %bitcast.8, s32[8]{0:T(128)} %quotas.1), custom_call_target="tpu_custom_call" | custom-call | tf_op jit(solution)/shard_map/pallas_call | solution.py:529
  126.2 1.6 %copy.11 = bf16[128,512]{1,0:T(8,128)(2,1)} copy(bf16[128,512]{1,0:T(8,128)(2,1)} %get-tuple-element.8) | data formatting | bytes 262144
  127.7 1.2 copy.12
